TPU v7x, 256 devices: a whole 4x4x8 slice. The times are simulated.
256 devices in a mesh: dp: 32 (over y, x, z_lo), mp: 8 (over z_hi, core).
Axes of the slice: x: 4, y: 4, z: 8 (z_hi: 4, z_lo: 2; z = z_hi * 2 + z_lo), core: 2. Of those that a mesh axis runs over, the one named last changes fastest.
Arguments:
- query: bfloat16 [2048, 4096], P('dp', 'mp'), may hold values from -144 to 144
- new_key: bfloat16 [2048, 4096], P('dp', 'mp'), may hold values from -6 to 6
- new_value: bfloat16 [2048, 4096], P('dp', 'mp'), may hold values from -6 to 6
- cache_key: bfloat16 [2048, 32, 16, 128], P('dp', 'mp'), may hold values from -6 to 6
- cache_value: bfloat16 [2048, 32, 16, 128], P('dp', 'mp'), may hold values from -6 to 6
- cache_len: int32 [2048], P('dp'), may hold values from 2 to 16
- residual: bfloat16 [2048, 8192], P('dp'), may hold values from -6 to 6
- out_weight: bfloat16 [4096, 8192], P('mp'), may hold values from -0.1875 to 0.1875
- norm_gain: bfloat16 [8192], P('mp'), may hold values from 0.25 to 1.75
- codec_weight: bfloat16 [8192, 1024], P('mp'), may hold values from -0.125 to 0.125
- finished: int32 [2048], P('dp'), may hold values from 0 to 1
- owner: int32 [2048], P('dp'), may hold values from 0 to 31, as said below
- frames: bfloat16 [32768, 1024], P('dp', 'mp'), may hold values from -6 to 6
- snake_alpha: float32 [1024], P('mp'), may hold values from 0.5 to 2
- filter_weight: bfloat16 [7, 1024, 1024], P(None, None, 'mp'), may hold values from -0.125 to 0.125
- conv_bias: float32 [1024], P('mp'), may hold values from -4 to 4
Outputs:
- hidden: bfloat16 [2048, 8192], P('dp', 'mp')
- audio: bfloat16 [32768, 1024], P('dp', 'mp')
Inputs may be any that keep to these rules, and one draw needn't show every extreme that they name: Within each aligned block of 64 rows, at most 4 finished rows name the same owner, and some owner is named by exactly 4 finished rows of the block.
All inputs are finite; a program needn't handle non-finite values.
Results may differ from a plain program's by a relative error of at most 0.0056.
Values may be sent and summed in bfloat16 or wider, within the bound.
No kernel may reach another device: no remote copies, remote signals or barrier semaphores. Data moves between devices by JAX's collectives and lax.ppermute only.
A program may use at most 128 MiB of HBM per device.

v0:
```python
import jax
import jax.numpy as jnp
from jax import lax
from jax.sharding import Mesh
from jax.sharding import PartitionSpec as P

KERNEL_TAPS = 7
DILATION_STEP = 3
CAP = 4
MP = ("mp_0", "mp_1")


def one_axis_at_a_time(x, axes):
    for axis in axes:
        x = lax.psum(x, axis)
    return x


def cut_along(x, dim, peers):
    before, after = (x.shape[:dim], x.shape[dim + 1 :])
    return jnp.moveaxis(x.reshape(*before, peers, -1, *after), dim, 0)


def sum_at_owner(x, axis, dim):
    peers = lax.axis_size(axis)
    pieces = lax.all_to_all(cut_along(x, dim, peers), axis, 0, 0, tiled=True)
    return jnp.sum(pieces, axis=0)


def padded(cells, sides, width):
    for axis, dim in sides:
        count = lax.axis_size(axis)
        ends = count - 1
        head = lax.slice_in_dim(cells, 0, width, axis=dim)
        tail = lax.slice_in_dim(cells, cells.shape[dim] - width, cells.shape[dim], axis=dim)
        cells = jnp.concatenate(
            [
                lax.ppermute(tail, axis, [(i, (i + 1) % count) for i in range(ends)]),
                cells,
                lax.ppermute(head, axis, [((i + 1) % count, i) for i in range(ends)]),
            ],
            axis=dim,
        )
    return cells


def attend(query, new_key, new_value, cache_key, cache_value, cache_len):
    count, heads, positions, depth = cache_key.shape
    scale = 1.0 / jnp.sqrt(jnp.float32(depth))
    queries = query.reshape(count, heads, depth)
    fresh_key = new_key.reshape(count, heads, depth)
    fresh_value = new_value.reshape(count, heads, depth)
    scores = (
        jnp.einsum("rhd,rhld->rhl", queries, cache_key, preferred_element_type=jnp.float32) * scale
    )
    own_score = (
        jnp.einsum("rhd,rhd->rh", queries, fresh_key, preferred_element_type=jnp.float32) * scale
    )
    valid = jnp.arange(positions, dtype=jnp.int32)[None, :] < cache_len[:, None]
    scores = jnp.where(valid[:, None, :], scores, -1e30)
    top = jnp.maximum(jnp.max(scores, axis=-1), own_score)
    expo = jnp.where(valid[:, None, :], jnp.exp(scores - top[..., None]), 0.0)
    own_expo = jnp.exp(own_score - top)
    total = jnp.sum(expo, axis=-1) + own_expo
    weights = (expo / total[..., None]).astype(jnp.bfloat16)
    own_weight = (own_expo / total).astype(jnp.bfloat16)
    mixed = jnp.einsum("rhl,rhld->rhd", weights, cache_value, preferred_element_type=jnp.float32)
    mixed = mixed + own_weight.astype(jnp.float32)[..., None] * fresh_value.astype(jnp.float32)
    return mixed.astype(jnp.bfloat16).reshape(count, heads * depth)


def body(
    query,
    new_key,
    new_value,
    cache_key,
    cache_value,
    cache_len,
    residual,
    out_weight,
    norm_gain,
    codec_weight,
    finished,
    owner,
    frames,
    snake_alpha,
    filter_weight,
    conv_bias,
):
    attended = attend(query, new_key, new_value, cache_key, cache_value, cache_len)
    count = attended.shape[0]
    width = out_weight.shape[1]
    local_width = norm_gain.shape[0]
    term = jnp.dot(attended, out_weight, preferred_element_type=jnp.float32)
    projected = lax.psum_scatter(term, MP, scatter_dimension=1, tiled=True)
    residual_part = lax.dynamic_slice_in_dim(
        residual, lax.axis_index(MP) * local_width, local_width, 1
    )
    hidden = (residual_part.astype(jnp.float32) + projected).astype(jnp.bfloat16)
    wide = hidden.astype(jnp.float32)
    squares = one_axis_at_a_time(jnp.sum(wide * wide, axis=-1), MP)
    meansq = squares / width
    normed = (wide * norm_gain.astype(jnp.float32)).astype(jnp.bfloat16)
    partial_value = jnp.dot(normed, codec_weight, preferred_element_type=jnp.float32)
    latent = sum_at_owner(partial_value, MP, 1)
    latent = (latent * lax.rsqrt(meansq + 1e-05)[:, None]).astype(jnp.bfloat16)
    owners = lax.axis_size("dp")
    index = jnp.arange(count, dtype=jnp.int32)
    earlier = (
        (owner[:, None] == owner[None, :])
        & (finished[None, :] == 1)
        & (index[None, :] < index[:, None])
    )
    slot = jnp.sum(earlier.astype(jnp.int32), axis=1)
    target = owner * CAP + slot
    places = jnp.arange(owners * CAP, dtype=jnp.int32)
    onehot = ((places[:, None] == target[None, :]) & (finished[None, :] == 1)).astype(jnp.bfloat16)
    outgoing = jnp.dot(onehot, latent, preferred_element_type=jnp.float32).astype(jnp.bfloat16)
    outgoing = outgoing.reshape(owners, CAP, latent.shape[1])
    incoming = lax.all_to_all(outgoing, "dp", split_axis=0, concat_axis=0, tiled=True)
    incoming = incoming.reshape(owners * CAP, latent.shape[1]).astype(jnp.float32)
    frame_tally = frames.shape[0]
    incoming = jnp.pad(incoming, ((0, frame_tally - owners * CAP), (0, 0)))
    mix = frames.astype(jnp.float32) + incoming
    act = (mix + jnp.sin(snake_alpha * mix) ** 2 / snake_alpha).astype(jnp.bfloat16)
    filter_span = KERNEL_TAPS // 2 * DILATION_STEP
    channels = lax.all_gather(act, MP, axis=1, tiled=True)
    padded_frames = padded(channels, (("dp", 0),), filter_span)
    dilated_filter = jnp.zeros(mix.shape, jnp.float32)
    for tap_index in range(KERNEL_TAPS):
        dilated_filter = dilated_filter + jnp.dot(
            padded_frames[tap_index * DILATION_STEP : tap_index * DILATION_STEP + frame_tally],
            filter_weight[tap_index],
            preferred_element_type=jnp.float32,
        )
    audio = (mix + conv_bias + dilated_filter).astype(jnp.bfloat16)
    return (hidden, audio)


def solution(mesh):
    torus = Mesh(mesh.devices.reshape(mesh.shape["dp"], 4, 2), ("dp", "mp_0", "mp_1"))
    return jax.shard_map(
        body,
        mesh=torus,
        in_specs=(
            P("dp", MP),
            P("dp", MP),
            P("dp", MP),
            P("dp", MP, None, None),
            P("dp", MP, None, None),
            P("dp"),
            P("dp", None),
            P(MP, None),
            P(MP),
            P(MP, None),
            P("dp"),
            P("dp"),
            P("dp", MP),
            P(MP),
            P(None, None, MP),
            P(MP),
        ),
        out_specs=(P("dp", MP), P("dp", MP)),
        check_vma=False,
    )
```

profile of v0, /device:TPU:8, one launch (start us, length us, event | category | flops | bytes accessed | tf_op | source)
XLA Modules:
  0.0 171.7 jit_solution(13440714838450825525)
XLA Ops:
  7.2 1.0 reshape.54
  8.3 0.9 reshape.67
  9.2 0.7 iota_compare_fusion.2
  9.8 0.9 reshape.55
  10.9 0.9 reshape.59
  11.8 1.9 %fusion.81 = f32[64,4,1,16]{3,2,1,0:T(1,128)S(1)} fusion(bf16[64,4,128,1]{2,3,1,0:T(2,128)(2,1)S(1)} %reshape.67, bf16[64,4,16,128]{3,2,1,0:T(8,128)(2,1)} %param.19), kind=kOutput, calls=%fused_computation.90 | convolution fusion | flops 1048576 | bytes 1130496 | tf_op jit(solution)/shard_map/rhd,rhld->rhl/dot_general | solution.py:54
  14.1 0.4 fusion.82
  14.7 6.3 %fusion.62 = f32[64,8192]{1,0:T(8,128)} fusion(bf16[512,8192]{1,0:T(8,128)(2,1)} %param.23, bf16[8,8,4,128]{3,2,1,0:T(4,128)(2,1)S(1)} %bitcast.60), kind=kOutput, calls=%fused_computation.56 | convolution fusion | flops 536870912 | bytes 10551296 | tf_op jit(solution)/shard_map/dot_general | solution.py:94
  21.0 0.6 copy-done.5
  21.7 45.6 %reduce-scatter.2.cloned.1.call-done = f32[64,1024]{1,0:T(8,128)} async-done(((f32[64,8192]{1,0:T(8,128)}), f32[64,1024]{1,0:T(8,128)}) %reduce-scatter.2.cloned.1.call-update) | async-done | bytes 262160 | tf_op jit(solution)/shard_map/reduce_scatter | solution.py:95
  67.3 1.1 fusion.43
  68.5 0.5 convolution_bitcast_fusion
  69.0 0.7 copy.37
  69.7 4.3 %all-to-all-start = ((f32[8,64,128]{2,1,0:T(8,128)}), f32[8,64,128]{2,1,0:T(8,128)S(1)}, u32[]{:S(2)}, u32[]{:S(2)}) async-start(f32[8,64,128]{2,1,0:T(8,128)} %bitcast.59), calls=%async_computation.1 | async-start | bytes 524288 | tf_op jit(solution)/shard_map/all_to_all | solution.py:26
  74.0 0.2 convert_reduce_fusion
  74.2 14.8 %psum.14 = f32[64]{0:T(128)S(1)} all-reduce(f32[64]{0:T(128)S(1)} %get-tuple-element.2), channel_id=1, replica_groups=mesh['dp'=32,'mp_0'=4,'mp_1'=2] {'mp_0'}, use_global_device_ids=true, to_apply=%region_6.7 | all-reduce | flops 64 | bytes 512 | tf_op jit(solution)/shard_map/psum | solution.py:15
  89.0 2.4 %psum.15 = f32[64]{0:T(128)S(1)} all-reduce(f32[64]{0:T(128)S(1)} %psum.14), channel_id=1, replica_groups=mesh['dp'=32,'mp_0'=4,'mp_1'=2] {'mp_1'}, use_global_device_ids=true, to_apply=%region_7.8 | all-reduce | flops 64 | bytes 512 | tf_op jit(solution)/shard_map/psum | solution.py:15
  91.5 0.2 convolution_convert_fusion
  91.7 15.0 %all_to_all.10 = bf16[32,4,128]{2,1,0:T(4,128)(2,1)S(1)} all-to-all(bf16[32,4,128]{2,1,0:T(4,128)(2,1)S(1)} %bitcast.63), channel_id=1, replica_groups=mesh['dp'=32,'mp_0'=4,'mp_1'=2] {'dp'}, dimensions={0} | all-to-all | bytes 65536 | tf_op jit(solution)/shard_map/all_to_all | solution.py:120
  106.7 2.5 %add_convert_fusion = bf16[1024,128]{1,0:T(8,128)(2,1)} fusion(bf16[1024,128]{1,0:T(8,128)(2,1)S(1)} %copy-done.3, bf16[128,128]{1,0:T(8,128)(2,1)S(1)} %bitcast.61, f32[128]{0:T(128)S(1)} %copy-done.7), kind=kLoop, calls=%fused_computation.29 | loop fusion | flops 1048576 | bytes 557568 | tf_op jit(solution)/shard_map/convert_element_type | solution.py:125
  109.3 36.8 %all-gather.2.cloned.1.call-done = bf16[1024,1024]{1,0:T(8,128)(2,1)} async-done(((bf16[1024,128]{1,0:T(8,128)(2,1)}), bf16[1024,1024]{1,0:T(8,128)(2,1)}) %all-gather.2.cloned.1.call-update) | async-done | bytes 2097168 | tf_op jit(solution)/shard_map/all_gather | solution.py:127
  146.0 0.9 fusion.80
  147.0 1.9 %collective-permute-start = (bf16[9,1024]{1,0:T(8,128)(2,1)S(1)}, bf16[9,1024]{1,0:T(8,128)(2,1)S(1)}, u32[]{:S(2)}, u32[]{:S(2)}) collective-permute-start(bf16[9,1024]{1,0:T(8,128)(2,1)S(1)} %get-tuple-element.4), channel_id=1, source_target_pairs={{0,8},{8,16},{16,24},{24,32},{32,40},{40,48},{48,56},{56,64},{64,7... | collective-permute-start | bytes 55304 | tf_op jit(solution)/shard_map/ppermute | solution.py:38
  148.9 6.9 %collective-permute-start.1 = (bf16[9,1024]{1,0:T(8,128)(2,1)S(1)}, bf16[9,1024]{1,0:T(8,128)(2,1)S(1)}, u32[]{:S(2)}, u32[]{:S(2)}) collective-permute-start(bf16[9,1024]{1,0:T(8,128)(2,1)S(1)} %get-tuple-element.5), channel_id=1, source_target_pairs={{8,0},{16,8},{24,16},{32,24},{40,32},{48,40},{56,48},{64,56},{72,6... | collective-permute-start | bytes 55304 | tf_op jit(solution)/shard_map/ppermute | solution.py:40
  155.8 2.3 %fusion.47 = f32[1024,128]{1,0:T(8,128)S(1)} fusion(bf16[1024,1024]{1,0:T(8,128)(2,1)} %all-gather.2.cloned.1.call-done, bf16[7,1024,128]{2,1,0:T(8,128)(2,1)} %param.30), kind=kOutput, calls=%fused_computation.39 | convolution fusion | flops 268435456 | bytes 2883584 | tf_op jit(solution)/shard_map/dot_general | solution.py:131
  158.4 1.3 copy-done.4
  159.7 0.7 fusion.8
  160.4 0.7 fusion.6
  161.1 0.7 fusion.12
  161.8 0.7 fusion.1
  162.6 0.7 fusion.36
  163.3 1.5 fusion.39
  (45 shorter events, 1.2 us)
Async XLA Ops:
  7.2 61.3 %copy-start = (bf16[1024,1024]{1,0:T(8,128)(2,1)S(1)}, bf16[1024,1024]{1,0:T(8,128)(2,1)}, u32[]{:S(2)}) copy-start(bf16[1024,1024]{1,0:T(8,128)(2,1)} %param.25) | copy-start | bytes 6291460
  7.2 6.9 %copy-start.8 = (bf16[64,4,16,128]{3,2,1,0:T(8,128)(2,1)S(1)}, bf16[64,4,16,128]{3,2,1,0:T(8,128)(2,1)}, u32[]{:S(2)}) copy-start(bf16[64,4,16,128]{3,2,1,0:T(8,128)(2,1)} %param.20) | copy-start | bytes 3145732
  7.2 60.1 %reduce-scatter.2.cloned.1.call-start = ((), (), s32[]{:S(2)}) async-start(), calls=%async_computation.3 | async-start | bytes 2359296 | tf_op jit(solution)/shard_map/reduce_scatter | solution.py:95
  21.0 0.7 copy-start.5
  21.0 0.7 copy-start.9
  21.0 53.0 %copy-start.6 = (s32[64]{0:T(128)S(1)}, s32[64]{0:T(128)}, u32[]{:S(2)}) copy-start(s32[64]{0:T(128)} %param.27) | copy-start | bytes 772
  68.4 40.8 %copy-start.2 = (bf16[64,1024]{1,0:T(8,128)(2,1)}, bf16[64,1024]{1,0:T(8,128)(2,1)S(1)}, u32[]{:S(2)}) copy-start(bf16[64,1024]{1,0:T(8,128)(2,1)S(1)} %get-tuple-element.3) | copy-start | bytes 393220
  68.4 38.3 %copy-start.3 = (bf16[1024,128]{1,0:T(8,128)(2,1)S(1)}, bf16[1024,128]{1,0:T(8,128)(2,1)}, u32[]{:S(2)}) copy-start(bf16[1024,128]{1,0:T(8,128)(2,1)} %param.28) | copy-start | bytes 786436
  68.4 38.3 %copy-start.7 = (f32[128]{0:T(128)S(1)}, f32[128]{0:T(128)}, u32[]{:S(2)}) copy-start(f32[128]{0:T(128)} %param.29) | copy-start | bytes 1540
  69.7 21.8 %all-to-all-start = ((f32[8,64,128]{2,1,0:T(8,128)}), f32[8,64,128]{2,1,0:T(8,128)S(1)}, u32[]{:S(2)}, u32[]{:S(2)}) async-start(f32[8,64,128]{2,1,0:T(8,128)} %bitcast.59), calls=%async_computation.1 | async-start | bytes 524288 | tf_op jit(solution)/shard_map/all_to_all | solution.py:26
  73.9 72.1 %all-gather.2.cloned.1.call-start = ((), (), s32[]{:S(2)}) async-start(), calls=%async_computation.4 | async-start | bytes 2359296 | tf_op jit(solution)/shard_map/all_gather | solution.py:127
  146.0 12.1 %copy-start.1 = (bf16[1024,1024]{1,0:T(8,128)(2,1)S(1)}, bf16[1024,1024]{1,0:T(8,128)(2,1)}, u32[]{:S(2)}) copy-start(bf16[1024,1024]{1,0:T(8,128)(2,1)} %all-gather.2.cloned.1.call-done) | copy-start | bytes 6291460
  147.0 14.1 %collective-permute-start = (bf16[9,1024]{1,0:T(8,128)(2,1)S(1)}, bf16[9,1024]{1,0:T(8,128)(2,1)S(1)}, u32[]{:S(2)}, u32[]{:S(2)}) collective-permute-start(bf16[9,1024]{1,0:T(8,128)(2,1)S(1)} %get-tuple-element.4), channel_id=1, source_target_pairs={{0,8},{8,16},{16,24},{24,32},{32,40},{40,48},{48,56},{56,64},{64,7... | collective-permute-start | bytes 55304 | tf_op jit(solution)/shard_map/ppermute | solution.py:38
  148.9 9.4 %collective-permute-start.1 = (bf16[9,1024]{1,0:T(8,128)(2,1)S(1)}, bf16[9,1024]{1,0:T(8,128)(2,1)S(1)}, u32[]{:S(2)}, u32[]{:S(2)}) collective-permute-start(bf16[9,1024]{1,0:T(8,128)(2,1)S(1)} %get-tuple-element.5), channel_id=1, source_target_pairs={{8,0},{16,8},{24,16},{32,24},{40,32},{48,40},{56,48},{64,56},{72,6... | collective-permute-start | bytes 55304 | tf_op jit(solution)/shard_map/ppermute | solution.py:40
  158.2 1.5 copy-start.4
  162.5 0.8 copy-start.10
Sparse Core Ops, SparseCore 0:
  21.2 46.0 reduce-scatter.1
  109.4 36.6 all-gather.1
where the time goes:
time: 172 us
  waiting for transfers between devices  82.4 us (48%)
  blocking collectives  32.3 us (19%)
  matrix products  16.7 us (10%)
  between operations  14.3 us (8%)
  starting transfers between devices  13.2 us (8%)
  local copies, waits for them, and re-layouts  7.87 us (5%)
  other arithmetic  4.9 us (3%)
    reduce_scatter x1, waiting for transfers between devices, body(): projected = lax.psum_scatter(term, MP, scatter_dimension=1, tiled=True)  45.6 us
    all_gather x1, waiting for transfers between devices, body(): channels = lax.all_gather(act, MP, axis=1, tiled=True)  36.8 us
    psum x2, blocking collectives, one_axis_at_a_time(): x = lax.psum(x, axis)  17.3 us
    all_to_all x1, blocking collectives, body(): lax.all_to_all(outgoing, 'dp', split_axis=0, concat_axis=0, tiled=True)  15 us
    dot_general x7, matrix products, body(): jnp.dot(padded_frames[tap_index * DILATION_STEP:tap_index * DILATION_STEP...  7.41 us
    ppermute x1, starting transfers between devices, padded(): lax.ppermute(head, axis, [((i + 1) % count, i) for i in range(ends)])  6.93 us
    dot_general x1, matrix products, body(): term = jnp.dot(attended, out_weight, preferred_element_type=jnp.float32)  6.31 us
    all_to_all x1, starting transfers between devices, sum_at_owner(): pieces = lax.all_to_all(cut_along(x, dim, peers), axis, 0, 0, tiled=True)  4.26 us
  transfers between devices with their start and end apart: 5, of which 2 were waited for; matrix products, arithmetic and copies ran while one was open for 2% of the time, Pallas kernels for 0%

commit v1 on v0

v1 whole, which is shorter than its diff:
```python
import math
import jax
import jax.numpy as jnp
from jax import lax
from jax.experimental import pallas as pl
from jax.experimental.pallas import tpu as pltpu
from jax.sharding import Mesh
from jax.sharding import PartitionSpec as P

TAPS = 7
STEP = 3
CAP = 4
ZH = 4
MP = ("zh", "c")
F32 = jnp.float32
BF16 = jnp.bfloat16
ORDER = (2, 1, 3, 0)
VM = pl.BlockSpec(memory_space=pltpu.VMEM)
ANY = pl.BlockSpec(memory_space=pl.ANY)
DMA = pltpu.SemaphoreType.DMA


def params(mib=8):
    return pltpu.CompilerParams(vmem_limit_bytes=mib * 1024 * 1024)


def sds(shape, dtype):
    return jax.ShapeDtypeStruct(shape, dtype)


def placed_in(x, space):
    return pltpu.with_memory_space_constraint(x, space)


def call(kernel, name, outs, ins, scratch=(), far=(), far_outs=(), mib=8, alias=None, cost=None):
    return pl.pallas_call(
        kernel,
        in_specs=[ANY if i in far else VM for i in range(len(ins))],
        out_specs=[ANY if i in far_outs else VM for i in range(len(outs))] if isinstance(outs, list) else ANY if far_outs else VM,
        out_shape=outs,
        scratch_shapes=list(scratch),
        input_output_aliases=alias or {},
        compiler_params=params(mib),
        cost_estimate=cost,
        name=name,
    )(*[placed_in(x, pltpu.HBM if i in far else pltpu.VMEM) for i, x in enumerate(ins)])


def work(us):
    return pl.CostEstimate(flops=int(us * 1e7), transcendentals=0, bytes_accessed=int(us * 3e4))


def iota(shape, dim):
    return lax.broadcasted_iota(jnp.int32, shape, dim)


def as_column(row, size):
    diag = iota((size, size), 0) == iota((size, size), 1)
    return jnp.sum(jnp.where(diag, jnp.broadcast_to(row, (size, size)), 0), axis=1, keepdims=True)


def sin_squared(x):
    k = jnp.floor(x * (1.0 / math.pi) + 0.5)
    r = x - k * 3.140625
    r = r - k * 9.67502593994140625e-4
    r = r - k * 1.509957990978376432e-7
    s = r * r
    p = -1.0 / 39916800.0
    p = p * s + 1.0 / 362880.0
    p = p * s - 1.0 / 5040.0
    p = p * s + 1.0 / 120.0
    p = p * s - 1.0 / 6.0
    y = r + r * (s * p)
    return y * y


def attend_kernel(
    q_hbm, nk_hbm, nv_hbm, ck_hbm, cv_hbm, len_hbm, fin_hbm, own_hbm, w_hbm,
    theirs_ref, att_ref, weight_ref, tgt_ref,
    q_ref, nk_ref, nv_ref, ck_ref, cv_ref, len_ref, fin_ref, own_ref, peer_ref, small_sem, key_sem, value_sem, peer_sem, own_sem,
):
    rows, heads, places, depth = ck_ref.shape
    group = 16
    groups = rows // group
    wide = group * places
    width = weight_ref.shape[2]
    chip, core = lax.axis_index("zh"), lax.axis_index("c")
    small = [
        pltpu.make_async_copy(src, dst, small_sem.at[i])
        for i, (src, dst) in enumerate(
            [(q_hbm, q_ref), (nk_hbm, nk_ref), (nv_hbm, nv_ref), (len_hbm, len_ref), (fin_hbm, fin_ref), (own_hbm, own_ref)]
        )
    ]
    keys, values, theirs, ours = [], [], [], []
    for g in range(groups):
        span = pl.ds(g * group, group)
        keys.append(pltpu.make_async_copy(ck_hbm.at[span], ck_ref.at[span], key_sem.at[g]))
        values.append(pltpu.make_async_copy(cv_hbm.at[span], cv_ref.at[span], value_sem.at[g]))
    for i, d in enumerate(ORDER):
        block = lax.rem(chip + d, ZH) * 2
        for held, to, sem, side in ((theirs, peer_ref, peer_sem, 1 - core), (ours, weight_ref, own_sem, core)):
            at = pl.multiple_of((block + side) * width, width)
            held.append(pltpu.make_async_copy(w_hbm.at[:, pl.ds(at, width)], to.at[i], sem.at[i]))
    for copy in small:
        copy.start()
    for g in range(groups):
        keys[g].start()
        values[g].start()
    for copy in theirs + ours:
        copy.start()
    for copy in small:
        copy.wait()
    scale = 1.0 / math.sqrt(depth)

    fin = fin_ref[...]
    owner = own_ref[...]
    fin_col = as_column(fin, rows)
    owner_col = as_column(owner, rows)
    earlier = (owner_col == owner) & (fin_col == 1) & (iota((rows, rows), 0) < iota((rows, rows), 1))
    slot = jnp.sum(earlier.astype(jnp.int32), axis=0, keepdims=True)
    done = fin == 1
    tgt_ref[0:1] = jnp.where(done, owner * (2 * CAP) + slot, -1)
    tgt_ref[1:2] = jnp.where(done & (owner >= 1), (owner - 1) * (2 * CAP) + CAP + slot, -1)

    length = as_column(len_ref[...], rows)
    offset = iota((group, wide), 1) - places * iota((group, wide), 0)
    for g in range(groups):
        span = slice(g * group, (g + 1) * group)
        inside = (offset >= 0) & (offset < length[span])
        valid = jnp.concatenate([inside.astype(F32)] * heads, axis=0) > 0.5
        keys[g].wait()
        scores, own = [], []
        for h in range(heads):
            cols = slice(h * depth, (h + 1) * depth)
            q = q_ref[span, cols]
            k = ck_ref[span, h].reshape(wide, depth)
            scores.append(lax.dot_general(q, k, (((1,), (1,)), ((), ())), preferred_element_type=F32))
            own.append(jnp.sum(q.astype(F32) * nk_ref[span, cols].astype(F32), axis=1, keepdims=True))
        scores = jnp.where(valid, jnp.concatenate(scores, axis=0) * scale, -1e30)
        own = jnp.concatenate(own, axis=0) * scale
        top = jnp.maximum(jnp.max(scores, axis=1, keepdims=True), own)
        expo = jnp.where(valid, jnp.exp(scores - top), 0.0)
        own_expo = jnp.exp(own - top)
        inv = 1.0 / (jnp.sum(expo, axis=1, keepdims=True) + own_expo)
        weights = (expo * inv).astype(BF16)
        own_weight = (own_expo * inv).astype(BF16).astype(F32)
        values[g].wait()
        for h in range(heads):
            cols = slice(h * depth, (h + 1) * depth)
            part = slice(h * group, (h + 1) * group)
            mixed = jnp.dot(weights[part], cv_ref[span, h].reshape(wide, depth), preferred_element_type=F32)
            att_ref[span, cols] = (mixed + own_weight[part] * nv_ref[span, cols].astype(F32)).astype(BF16)
    att = att_ref[...]
    for i in range(ZH):
        theirs[i].wait()
        theirs_ref[i] = jnp.dot(att, peer_ref[i], preferred_element_type=F32).astype(BF16)
    for copy in ours:
        copy.wait()


def attend(query, new_key, new_value, cache_key, cache_value, cache_len, finished, owner, weight, width):
    rows = query.shape[0]
    depth = weight.shape[0]
    line = lambda x: x.reshape(1, rows)
    ins = (query, new_key, new_value, cache_key, cache_value, line(cache_len), line(finished), line(owner), weight)
    dma = DMA
    return call(
        attend_kernel,
        "attend",
        [
            pltpu.VMEM((ZH, rows, width), BF16),
            pltpu.VMEM((rows, depth), BF16),
            pltpu.VMEM((ZH, depth, width), BF16),
            pltpu.VMEM((2, rows), jnp.int32),
        ],
        ins,
        scratch=[pltpu.VMEM(x.shape, x.dtype) for x in ins[:8]]
        + [pltpu.VMEM((ZH, depth, width), BF16), dma((6,)), dma((rows // 16,)), dma((rows // 16,)), dma((ZH,)), dma((ZH,))],
        far=range(9),
        mib=16,
        cost=work(6),
    )


def project_kernel(att_ref, w_ref, res_hbm, codec_hbm, gain_hbm, out_ref, codec_ref, gain_ref, res_ref, line_ref, sems):
    width = w_ref.shape[2]
    at = pl.multiple_of((lax.axis_index("zh") * 2 + lax.axis_index("c")) * width, width)
    res_copy = pltpu.make_async_copy(res_hbm.at[:, pl.ds(at, width)], res_ref, sems.at[0])
    gain_copy = pltpu.make_async_copy(gain_hbm, line_ref, sems.at[1])
    codec_copy = pltpu.make_async_copy(codec_hbm, codec_ref, sems.at[2])
    res_copy.start()
    gain_copy.start()
    codec_copy.start()
    att = att_ref[...]
    for i, d in enumerate(ORDER):
        part = jnp.dot(att, w_ref[i], preferred_element_type=F32)
        if d == 0:
            res_copy.wait()
            part = part + res_ref[...].astype(F32)
        out_ref[i] = part
    gain_copy.wait()
    gain_ref[...] = line_ref[...].astype(F32).reshape(1, width)
    codec_copy.wait()


def project(attended, weight, residual, codec, gain):
    rows = attended.shape[0]
    count, _, width = weight.shape
    return call(
        project_kernel,
        "project",
        [pltpu.VMEM((count, rows, width), F32), pltpu.VMEM(codec.shape, BF16), pltpu.VMEM((1, width), F32)],
        (attended, weight, residual, codec, gain),
        scratch=[pltpu.VMEM((rows, width), BF16), pltpu.VMEM(gain.shape, BF16), DMA((3,))],
        far=(2, 3, 4),
        cost=work(2),
    )


def pair_kernel(own_ref, peer_ref, *outs):
    for i, out in enumerate(outs):
        out[...] = (own_ref[i] + peer_ref[i].astype(F32)).astype(BF16)


def pair(own, peer):
    _, rows, width = own.shape
    return call(pair_kernel, "pair", [pltpu.VMEM((rows, width), BF16)] * (ZH - 1), (own, peer), cost=work(0.5))


def split_sum(total):
    hi = total.astype(BF16).astype(F32)
    lo = total - hi
    lane = iota((total.shape[0], 128), 1)
    return jnp.where(lane == 0, hi, jnp.where(lane == 1, lo, 0.0)).astype(BF16)


def hidden_kernel(own_ref, peer_ref, r2_ref, r1_ref, r3_ref, gain_ref, codec_ref, hid_ref, keep_ref, send_ref):
    half = codec_ref.shape[1] // 2
    last = ORDER.index(0)
    total = own_ref[last] + peer_ref[last].astype(F32)
    total = total + r2_ref[...].astype(F32) + (r1_ref[...].astype(F32) + r3_ref[...].astype(F32))
    hidden = total.astype(BF16)
    hid_ref[...] = hidden
    wide = hidden.astype(F32)
    normed = (wide * gain_ref[...]).astype(BF16)
    squares = jnp.sum(wide * wide, axis=1, keepdims=True)
    part = jnp.dot(normed, codec_ref[...], preferred_element_type=F32)
    left, right = part[:, :half], part[:, half:]
    first = lax.axis_index("c") == 0
    keep_ref[:, :half] = jnp.where(first, left, right)
    send_ref[:, :half] = jnp.where(first, right, left).astype(BF16)
    keep_ref[:, half:] = jnp.broadcast_to(squares, (squares.shape[0], 128))
    send_ref[:, half:] = split_sum(squares)


def hidden_step(own, peer, r2, r1, r3, gain, codec):
    rows, width = r2.shape
    ext = codec.shape[1] // 2 + 128
    outs = [pltpu.VMEM((rows, width), BF16), pltpu.VMEM((rows, ext), F32), pltpu.VMEM((rows, ext), BF16)]
    return call(hidden_kernel, "hidden", outs, (own, peer, r2, r1, r3, gain, codec), cost=work(2))


def join_kernel(keep_ref, recv_ref, out_ref):
    half = keep_ref.shape[1] - 128
    recv = recv_ref[...].astype(F32)
    out_ref[:, :half] = (keep_ref[:, :half] + recv[:, :half]).astype(BF16)
    squares = keep_ref[:, half : half + 1] + recv[:, half : half + 1] + recv[:, half + 1 : half + 2]
    out_ref[:, half:] = split_sum(squares)


def join(keep, recv):
    return call(join_kernel, "join", pltpu.VMEM(recv.shape, BF16), (keep, recv), cost=work(0.3))


def dispatch_kernel(features, a_ref, b_ref, c_ref, d_ref, tgt_ref, out_ref):
    half = a_ref.shape[1] - 128
    owners, slots, _ = out_ref.shape
    rows = a_ref.shape[0]
    total = (a_ref[...].astype(F32) + b_ref[...].astype(F32)) + (c_ref[...].astype(F32) + d_ref[...].astype(F32))
    squares = total[:, half : half + 1] + total[:, half + 1 : half + 2]
    latent = (total[:, :half] * lax.rsqrt(squares / features + 1e-05)).astype(BF16)
    place = iota((owners * slots, rows), 0)
    onehot = ((place == tgt_ref[0:1]) | (place == tgt_ref[1:2])).astype(F32).astype(BF16)
    placed = jnp.dot(onehot, latent, preferred_element_type=F32)
    out_ref[...] = placed.reshape(owners, slots, half).astype(BF16)


def dispatch(features, owners, parts, targets):
    half = parts[0].shape[1] - 128
    kernel = lambda *refs: dispatch_kernel(features, *refs)
    return call(kernel, "dispatch", pltpu.VMEM((owners, 2 * CAP, half), BF16), (*parts, targets), cost=work(1))


def payload_kernel(frames_hbm, alpha_hbm, out_ref, frames_ref, alpha_ref, sems):
    copies = [
        pltpu.make_async_copy(alpha_hbm, alpha_ref, sems.at[0]),
        pltpu.make_async_copy(frames_hbm, frames_ref, sems.at[1]),
    ]
    for copy in copies:
        copy.start()
    for copy in copies:
        copy.wait()
    count, width = frames_ref.shape
    first = out_ref.shape[0] - count
    raw = frames_ref[...]
    early = 32 * CAP
    alpha = alpha_ref[...]
    mix = raw[early:].astype(F32)
    act = mix + sin_squared(alpha * mix) * (1.0 / alpha)
    out_ref[0:early] = raw[:early]
    out_ref[early:count] = act.astype(BF16)
    hi = alpha.astype(BF16).astype(F32)
    mid = (alpha - hi).astype(BF16).astype(F32)
    lo = alpha - hi - mid
    row = iota((first, width), 0)
    out_ref[count:] = jnp.where(row == 0, hi, jnp.where(row == 1, mid, jnp.where(row == 2, lo, 0.0))).astype(BF16)


def payload(frames, alpha):
    count, width = frames.shape
    return call(
        payload_kernel,
        "payload",
        pltpu.VMEM((count + 16, width), BF16),
        (frames, alpha.reshape(1, width)),
        scratch=[pltpu.VMEM((count, width), BF16), pltpu.VMEM((1, width), F32), DMA((2,))],
        far=(0, 1),
        cost=work(1.5),
    )


HEAD = 32 * CAP
EDGE = 16
TOP = HEAD + EDGE


def taps_sum(y, base, count):
    total = None
    for t in range(TAPS):
        at = base + (t - TAPS // 2) * STEP
        part = y[at : at + count, t * 128 : (t + 1) * 128]
        total = part if total is None else total + part
    return total


CUT = 512


def main_kernel(*refs):
    pieces = refs[:10]
    filt_hbm, own_hbm, bias_hbm, audio_hbm, raw_ref, alpha_ref, near_ref, tail_ref, wcat_ref, ends_ref, bias_ref = refs[10:21]
    act_ref, y_ref, own_ref, out_ref, sems = refs[21:]
    chip, core = lax.axis_index("zh"), lax.axis_index("c")
    copies = [
        pltpu.make_async_copy(filt_hbm.at[t], wcat_ref.at[:, pl.ds(t * 128, 128)], sems.at[t]) for t in range(TAPS)
    ]
    copies.append(pltpu.make_async_copy(own_hbm, own_ref, sems.at[TAPS]))
    copies.append(pltpu.make_async_copy(bias_hbm, bias_ref, sems.at[TAPS + 1]))
    for copy in copies:
        copy.start()
    count = own_ref.shape[0]
    for k in range(8):
        source = lax.rem(chip + k // 2, ZH) * 2 + (core if k % 2 == 0 else 1 - core)
        cols = pl.ds(pl.multiple_of(source * 128, 128), 128)
        if k // 2 == 2:
            head, rest = pieces[4 + k % 2], pieces[6 + k % 2]
            act_ref[0 : CUT - HEAD, cols] = head[HEAD:CUT]
            act_ref[CUT - HEAD :, cols] = rest[0 : count - CUT]
            extra = rest[count - CUT :]
        else:
            head = pieces[k if k < 4 else k + 2]
            act_ref[:, cols] = head[HEAD:count]
            extra = head[count : count + 16]
        raw_ref[:, cols] = head[0:HEAD]
        extra = extra.astype(F32)
        alpha_ref[:, cols] = jnp.broadcast_to(extra[0:1] + extra[1:2] + extra[2:3], (8, 128))
    near_ref[...] = act_ref[0 : 2 * EDGE]
    tail_ref[...] = act_ref[count - HEAD - 2 * EDGE : count - HEAD]
    for copy in copies:
        copy.wait()
    y_ref[...] = jnp.dot(act_ref[...], wcat_ref[...], preferred_element_type=F32)
    inner = count - TOP - EDGE
    conv = taps_sum(y_ref, EDGE, inner)
    mix = own_ref[TOP : TOP + inner].astype(F32)
    out_ref[...] = (mix + bias_ref[...] + conv).astype(BF16)
    ends_ref[0:TOP] = own_ref[0:TOP]
    ends_ref[TOP:] = own_ref[count - EDGE : count]
    last = pltpu.make_async_copy(out_ref, audio_hbm.at[pl.ds(TOP, inner)], sems.at[TAPS + 2])
    last.start()
    last.wait()


def main_conv(pieces, filt, frames, bias):
    count, width = frames.shape
    taps, channels, _ = filt.shape
    outs = [
        pltpu.HBM((count, width), BF16),
        pltpu.VMEM((HEAD, channels), BF16),
        pltpu.VMEM((8, channels), F32),
        pltpu.VMEM((2 * EDGE, channels), BF16),
        pltpu.VMEM((2 * EDGE, channels), BF16),
        pltpu.VMEM((channels, taps * width), BF16),
        pltpu.VMEM((TOP + EDGE, width), BF16),
        pltpu.VMEM((1, width), F32),
    ]
    scratch = [
        pltpu.VMEM((count - HEAD, channels), BF16),
        pltpu.VMEM((count - HEAD, taps * width), F32),
        pltpu.VMEM((count, width), BF16),
        pltpu.VMEM((count - TOP - EDGE, width), BF16),
        DMA((TAPS + 3,)),
    ]
    ins = (*pieces, filt, frames, bias.reshape(1, width))
    return call(main_kernel, "main_conv", outs, ins, scratch, far=(10, 11, 12), far_outs=(0,), mib=16, cost=work(4))


def final_kernel(
    mine_ref, peer_ref, raw_ref, alpha_ref, near_ref, tail_ref, before_ref, after_ref, wcat_ref, ends_ref, bias_ref, audio_ref,
    out_ref, act_ref, y_ref, out_top_ref, out_low_ref, top_sem, low_sem,
):
    del audio_ref
    core, chip = lax.axis_index("c"), lax.axis_index("zh")
    owners, slots, half = mine_ref.shape
    count = out_ref.shape[0]
    places = owners * slots
    first = core == 0
    mine = mine_ref[...].astype(F32).reshape(places, half)
    peer = peer_ref[...].astype(F32).reshape(places, half)
    left = jnp.where(first, mine, peer).astype(BF16)
    right = jnp.where(first, peer, mine).astype(BF16)
    row = iota((HEAD + EDGE, places), 0)
    place = iota((HEAD + EDGE, places), 1)
    own_place = (row // CAP) * slots + row % CAP
    after = row - HEAD
    after_place = (after // CAP) * slots + CAP + after % CAP
    pick = (place == jnp.where(row < HEAD, own_place, after_place)).astype(F32).astype(BF16)
    alpha = alpha_ref[0:1]
    inv = 1.0 / alpha
    taken = []
    for k, side in ((0, left), (1, right)):
        cols = slice(k * half, (k + 1) * half)
        got = jnp.dot(pick, side, preferred_element_type=F32)
        taken.append(got[:HEAD])
        mix = raw_ref[:, cols].astype(F32) + got[:HEAD]
        act_ref[EDGE : EDGE + HEAD, cols] = (mix + sin_squared(alpha[:, cols] * mix) * inv[:, cols]).astype(BF16)
        mix = after_ref[:, cols].astype(F32) + got[HEAD:]
        act_ref[EDGE + HEAD + 4 * EDGE :, cols] = (mix + sin_squared(alpha[:, cols] * mix) * inv[:, cols]).astype(BF16)
    act_ref[0:EDGE] = before_ref[EDGE:]
    act_ref[EDGE + HEAD : EDGE + HEAD + 2 * EDGE] = near_ref[...]
    act_ref[EDGE + HEAD + 2 * EDGE : EDGE + HEAD + 4 * EDGE] = tail_ref[...]
    y_ref[...] = jnp.dot(act_ref[...], wcat_ref[...], preferred_element_type=F32)
    bias = bias_ref[...]
    width = bias.shape[1]
    got = taken[0][:, 0:width]
    for k in range(1, 2 * half // width):
        at = k * width % half
        got = jnp.where(chip * 2 + core == k, taken[k * width // half][:, at : at + width], got)
    conv = taps_sum(y_ref, EDGE, TOP)
    mix = ends_ref[0:TOP].astype(F32)
    out_top_ref[0:HEAD] = (mix[:HEAD] + got + bias + conv[:HEAD]).astype(BF16)
    out_top_ref[HEAD:] = (mix[HEAD:] + bias + conv[HEAD:]).astype(BF16)
    conv = taps_sum(y_ref, EDGE + HEAD + 3 * EDGE, EDGE)
    out_low_ref[...] = (ends_ref[TOP:].astype(F32) + bias + conv).astype(BF16)
    top_copy = pltpu.make_async_copy(out_top_ref, out_ref.at[0:TOP], top_sem)
    low_copy = pltpu.make_async_copy(out_low_ref, out_ref.at[count - EDGE : count], low_sem)
    top_copy.start()
    low_copy.start()
    top_copy.wait()
    low_copy.wait()


def final_conv(mine, peer, raw, alpha, near, tail, before, after, wcat, ends, bias, audio):
    count, width = audio.shape
    channels = raw.shape[1]
    stack = EDGE + HEAD + 5 * EDGE
    return call(
        final_kernel,
        "final_conv",
        pltpu.HBM((count, width), BF16),
        (mine, peer, raw, alpha, near, tail, before, after, wcat, ends, bias, audio),
        scratch=[
            pltpu.VMEM((stack, channels), BF16),
            pltpu.VMEM((stack, TAPS * width), F32),
            pltpu.VMEM((TOP, width), BF16),
            pltpu.VMEM((EDGE, width), BF16),
            DMA,
            DMA,
        ],
        far=(11,),
        far_outs=(0,),
        mib=16,
        alias={11: 0},
        cost=work(3),
    )


def rotate(x, d):
    return lax.ppermute(x, "zh", [(i, (i + d) % ZH) for i in range(ZH)])


def swap(x):
    return lax.ppermute(x, "c", [(0, 1), (1, 0)])


def after_all(x, *tokens):
    return lax.optimization_barrier((x, *tokens))[0]


def body(
    query, new_key, new_value, cache_key, cache_value, cache_len, residual, out_weight, norm_gain, codec_weight,
    finished, owner, frames, snake_alpha, filter_weight, conv_bias,
):
    owners = lax.axis_size("dp")
    width = norm_gain.shape[0]

    sent = payload(frames, snake_alpha)
    left, right = rotate(sent, 1), rotate(sent, 3)
    query = after_all(query, sent)
    theirs, attended, weight, targets = attend(
        query, new_key, new_value, cache_key, cache_value, cache_len, finished, owner, out_weight, width
    )
    peer = swap(theirs)
    own, codec, gain = project(attended, weight, residual, codec_weight, norm_gain)
    got = {d: rotate(x, d) for d, x in zip(ORDER, pair(own, peer))}
    hidden, keep, send = hidden_step(own, peer, got[2], got[1], got[3], gain, codec)

    far_head = rotate(after_all(left[:CUT], hidden), 1)
    far_rest = rotate(after_all(right[CUT:], hidden), 3)
    pieces = []
    for x in (sent, right, far_head, far_rest, left):
        pieces += [x, swap(x)]

    joined = join(keep, swap(send))
    parts = [joined] + [rotate(joined, d) for d in (2, 1, 3)]
    audio, raw, alpha, close, tail, wcat, ends, bias = main_conv(pieces, filter_weight, frames, conv_bias)
    before = lax.ppermute(tail, "dp", [(i, i + 1) for i in range(owners - 1)])
    after = lax.ppermute(raw[:EDGE], "dp", [(i + 1, i) for i in range(owners - 1)])
    targets = after_all(targets, tail)
    outgoing = dispatch(residual.shape[1], owners, parts, targets)
    incoming = lax.all_to_all(outgoing, "dp", 0, 0, tiled=True)
    other = swap(incoming)
    audio = final_conv(incoming, other, raw, alpha, close, tail, before, after, wcat, ends, bias, audio)
    return (hidden, audio)


def solution(mesh):
    torus = Mesh(mesh.devices.reshape(mesh.shape["dp"], ZH, 2), ("dp", "zh", "c"))
    return jax.shard_map(
        body,
        mesh=torus,
        in_specs=(
            P("dp", MP), P("dp", MP), P("dp", MP), P("dp", MP, None, None), P("dp", MP, None, None), P("dp"), P("dp", None),
            P(MP, None), P(MP), P(MP, None), P("dp"), P("dp"), P("dp", MP), P(MP), P(None, None, MP), P(MP),
        ),
        out_specs=(P("dp", MP), P("dp", MP)),
        check_vma=False,
    )
```

time: 172 us -> 99.1 us (0.58)
  waiting for transfers between devices: 82.4 us -> 28.2 us
  starting transfers between devices: 13.2 us -> 32.5 us
  Pallas kernels: 0 us -> 18.3 us
  matrix products: 16.7 us -> 0 us
  blocking collectives: 32.3 us -> 16.9 us
  between operations: 14.3 us -> 0.94 us
  local copies, waits for them, and re-layouts: 7.87 us -> 0.68 us
  other arithmetic: 4.9 us -> 0 us
    reduce_scatter x1 -> x0, waiting for transfers between devices: 45.6 us -> none  [body(): projected = lax.psum_scatter(term, MP, scatter_dimension=1, tiled=True)]
    all_gather x1 -> x0, waiting for transfers between devices: 36.8 us -> none  [body(): channels = lax.all_gather(act, MP, axis=1, tiled=True)]
    ppermute x2 -> x20, waiting for transfers between devices: 0.01 us -> 28.2 us  [the longest x10 27.2 us: rotate(): return lax.ppermute(x, 'zh', [(i, (i + d) % ZH) for i in range(ZH)])]
    ppermute x2 -> x20, starting transfers between devices: 8.85 us -> 32.5 us  [the longest x10 22.5 us: rotate(): return lax.ppermute(x, 'zh', [(i, (i + d) % ZH) for i in range(ZH)])]
    pallas_call x0 -> x9, Pallas kernels: none -> 18.3 us  [call(): pl.pallas_call(kernel, in_specs=[ANY if i in far else VM for i in range(l...]
    psum x2 -> x0, blocking collectives: 17.3 us -> none  [one_axis_at_a_time(): x = lax.psum(x, axis)]
    dot_general x12 -> x0, matrix products: 16.7 us -> none  [the longest x7 7.41 us: body(): jnp.dot(padded_frames[tap_index * DILATION_STEP:tap_index * DILATION_STEP...]
    all_to_all x1 -> x0, starting transfers between devices: 4.26 us -> none  [sum_at_owner(): pieces = lax.all_to_all(cut_along(x, dim, peers), axis, 0, 0, tiled=True)]
  transfers between devices with their start and end apart: 5 -> 20, of which waited for: 2 -> 8; matrix products, arithmetic and copies ran while one was open for 2% -> 1% of each run, Pallas kernels for 0% -> 7%
where the time goes in v1:
time: 99.1 us; the launch traced here: 97.5 us
  starting transfers between devices  32.5 us (33%)
  waiting for transfers between devices  28.2 us (28%)
  Pallas kernels  18.3 us (18%)
  blocking collectives  16.9 us (17%)
    ppermute x10, waiting for transfers between devices, rotate(): return lax.ppermute(x, 'zh', [(i, (i + d) % ZH) for i in range(ZH)])  27.2 us
    ppermute x10, starting transfers between devices, rotate(): return lax.ppermute(x, 'zh', [(i, (i + d) % ZH) for i in range(ZH)])  22.5 us
    pallas_call x9, Pallas kernels, call(): pl.pallas_call(kernel, in_specs=[ANY if i in far else VM for i in range(l...  18.3 us
    all_to_all x1, blocking collectives, body(): incoming = lax.all_to_all(outgoing, 'dp', 0, 0, tiled=True)  16.9 us
    ppermute x1, starting transfers between devices, body(): lax.ppermute(raw[:EDGE], 'dp', [(i + 1, i) for i in range(owners - 1)])  5.5 us
    ppermute x1, starting transfers between devices, body(): before = lax.ppermute(tail, 'dp', [(i, i + 1) for i in range(owners - 1)])  3.34 us
  transfers between devices with their start and end apart: 20, of which 8 were waited for; matrix products, arithmetic and copies ran while one was open for 1% of the time, Pallas kernels for 7%

profile of v1, /device:TPU:8, one launch (start us, length us, event | category | flops | bytes accessed | tf_op | source)
XLA Modules:
  0.0 97.5 jit_solution(12877245748236996353)
XLA Ops:
  0.6 1.4 %payload.1.refs_0_ = bf16[1040,128]{1,0:T(8,128)(2,1)S(1)} custom-call(bf16[1024,128]{1,0:T(8,128)(2,1)} %refs_11_.1, f32[1,128]{1,0:T(1,128)} %bitcast.5), custom_call_target="tpu_custom_call" | custom-call | flops 15000000 | bytes 45000 | tf_op jit(solution)/shard_map/payload/pallas_call | solution.py:36
  2.0 7.3 %attend.1 = (bf16[4,64,1024]{2,1,0:T(8,128)(2,1)S(1)}, bf16[64,512]{1,0:T(8,128)(2,1)S(1)}, bf16[4,512,1024]{2,1,0:T(8,128)(2,1)S(1)}, s32[2,64]{1,0:T(2,128)S(1)}) custom-call(bf16[64,512]{1,0:T(8,128)(2,1)} %q_hbm, bf16[64,512]{1,0:T(8,128)(2,1)} %nk_hbm.1, bf16[64,512]{1,0:T(8,128)(2,1)} %nv_hbm.1, bf16[64,4,16,128]{3,2,1,0:T(8,128)(2,1)} %ck_hbm.1, ...), custom_call_target="tpu_custom_call" | custom-call | flops 60000000 | bytes 180000 | tf_op jit(solution)/shard_map/attend/pallas_call | solution.py:36
  9.4 6.4 %collective-permute-start.9 = (bf16[1040,128]{1,0:T(8,128)(2,1)S(1)}, bf16[1040,128]{1,0:T(8,128)(2,1)S(1)}, u32[]{:S(2)}, u32[]{:S(2)}) collective-permute-start(bf16[1040,128]{1,0:T(8,128)(2,1)S(1)} %payload.1.refs_0_), channel_id=1, source_target_pairs={{0,6},{2,0},{4,2},{6,4},{1,7},{3,1},{5,3},{7,5},{8,14},{10,8},{12,... | collective-permute-start | bytes 798728 | tf_op jit(solution)/shard_map/ppermute | solution.py:498
  15.8 2.2 %project.1 = (f32[4,64,1024]{2,1,0:T(8,128)S(1)}, bf16[1024,1024]{1,0:T(8,128)(2,1)S(1)}, f32[1,1024]{1,0:T(1,128)S(1)}) custom-call(bf16[64,512]{1,0:T(8,128)(2,1)S(1)} %get-tuple-element.28.att_ref, bf16[4,512,1024]{2,1,0:T(8,128)(2,1)S(1)} %get-tuple-element.29.w_ref, bf16[64,8192]{1,0:T(8,128)(2,1)} %res_hbm.1, bf16[1024,1024]{1,0:T(8,128)(2,1)} %codec_hbm.1, ...), custom_call_target="tpu_custom_call" | custom-call | flops 20000000 | bytes 60000 | tf_op jit(solution)/shard_map/project/pallas_call | solution.py:36
  18.1 3.9 %collective-permute-start.1 = (bf16[64,1024]{1,0:T(8,128)(2,1)S(1)}, bf16[64,1024]{1,0:T(8,128)(2,1)S(1)}, u32[]{:S(2)}, u32[]{:S(2)}) collective-permute-start(bf16[64,1024]{1,0:T(8,128)(2,1)S(1)} %get-tuple-element.32), channel_id=1, source_target_pairs={{0,4},{2,6},{4,0},{6,2},{1,5},{3,7},{5,1},{7,3},{8,12},{10,14},{12... | collective-permute-start | bytes 393224 | tf_op jit(solution)/shard_map/ppermute | solution.py:498
  22.0 2.7 %collective-permute-start.2 = (bf16[64,1024]{1,0:T(8,128)(2,1)S(1)}, bf16[64,1024]{1,0:T(8,128)(2,1)S(1)}, u32[]{:S(2)}, u32[]{:S(2)}) collective-permute-start(bf16[64,1024]{1,0:T(8,128)(2,1)S(1)} %get-tuple-element.33), channel_id=1, source_target_pairs={{0,2},{2,4},{4,6},{6,0},{1,3},{3,5},{5,7},{7,1},{8,10},{10,12},{12... | collective-permute-start | bytes 393224 | tf_op jit(solution)/shard_map/ppermute | solution.py:498
  24.6 1.5 %collective-permute-start.3 = (bf16[64,1024]{1,0:T(8,128)(2,1)S(1)}, bf16[64,1024]{1,0:T(8,128)(2,1)S(1)}, u32[]{:S(2)}, u32[]{:S(2)}) collective-permute-start(bf16[64,1024]{1,0:T(8,128)(2,1)S(1)} %get-tuple-element.34), channel_id=1, source_target_pairs={{0,6},{2,0},{4,2},{6,4},{1,7},{3,1},{5,3},{7,5},{8,14},{10,8},{12,... | collective-permute-start | bytes 393224 | tf_op jit(solution)/shard_map/ppermute | solution.py:498
  26.1 8.8 %collective-permute-done.1.r2_ref = bf16[64,1024]{1,0:T(8,128)(2,1)S(1)} collective-permute-done((bf16[64,1024]{1,0:T(8,128)(2,1)S(1)}, bf16[64,1024]{1,0:T(8,128)(2,1)S(1)}, u32[]{:S(2)}, u32[]{:S(2)}) %collective-permute-start.1) | collective-permute-done | bytes 131104 | tf_op jit(solution)/shard_map/ppermute | solution.py:498
  34.9 7.9 %collective-permute-done.2.r1_ref = bf16[64,1024]{1,0:T(8,128)(2,1)S(1)} collective-permute-done((bf16[64,1024]{1,0:T(8,128)(2,1)S(1)}, bf16[64,1024]{1,0:T(8,128)(2,1)S(1)}, u32[]{:S(2)}, u32[]{:S(2)}) %collective-permute-start.2) | collective-permute-done | bytes 131104 | tf_op jit(solution)/shard_map/ppermute | solution.py:498
  42.9 0.5 hidden.1
  43.5 0.5 collective-permute-start.8
  44.0 0.1 collective-permute-start.10
  44.1 0.4 collective-permute-start.16
  44.5 0.8 collective-permute-start.14
  45.3 2.3 %collective-permute-start.12 = (bf16[512,128]{1,0:T(8,128)(2,1)S(1)}, bf16[512,128]{1,0:T(8,128)(2,1)S(1)}, u32[]{:S(2)}, u32[]{:S(2)}) collective-permute-start(bf16[512,128]{1,0:T(8,128)(2,1)S(1)} %slice.12), channel_id=1, source_target_pairs={{0,2},{2,4},{4,6},{6,0},{1,3},{3,5},{5,7},{7,1},{8,10},{10,12},{12... | collective-permute-start | bytes 393224 | tf_op jit(solution)/shard_map/ppermute | solution.py:498
  47.6 6.4 %collective-permute-done.14.refs_6_ = bf16[528,128]{1,0:T(8,128)(2,1)S(1)} collective-permute-done((bf16[528,128]{1,0:T(8,128)(2,1)S(1)}, bf16[528,128]{1,0:T(8,128)(2,1)S(1)}, u32[]{:S(2)}, u32[]{:S(2)}) %collective-permute-start.14) | collective-permute-done | bytes 135200 | tf_op jit(solution)/shard_map/ppermute | solution.py:498
  54.0 1.5 %collective-permute-done.12.refs_4_ = bf16[512,128]{1,0:T(8,128)(2,1)S(1)} collective-permute-done((bf16[512,128]{1,0:T(8,128)(2,1)S(1)}, bf16[512,128]{1,0:T(8,128)(2,1)S(1)}, u32[]{:S(2)}, u32[]{:S(2)}) %collective-permute-start.12) | collective-permute-done | bytes 131104 | tf_op jit(solution)/shard_map/ppermute | solution.py:498
  55.5 0.2 join.1.refs_0_
  55.7 0.3 collective-permute-start.5
  56.0 3.2 %collective-permute-start.6 = (bf16[64,640]{1,0:T(8,128)(2,1)S(1)}, bf16[64,640]{1,0:T(8,128)(2,1)S(1)}, u32[]{:S(2)}, u32[]{:S(2)}) collective-permute-start(bf16[64,640]{1,0:T(8,128)(2,1)S(1)} %join.1.refs_0_), channel_id=1, source_target_pairs={{0,2},{2,4},{4,6},{6,0},{1,3},{3,5},{5,7},{7,1},{8,10},{10,12},{12... | collective-permute-start | bytes 245768 | tf_op jit(solution)/shard_map/ppermute | solution.py:498
  59.2 1.4 %collective-permute-start.7 = (bf16[64,640]{1,0:T(8,128)(2,1)S(1)}, bf16[64,640]{1,0:T(8,128)(2,1)S(1)}, u32[]{:S(2)}, u32[]{:S(2)}) collective-permute-start(bf16[64,640]{1,0:T(8,128)(2,1)S(1)} %join.1.refs_0_), channel_id=1, source_target_pairs={{0,6},{2,0},{4,2},{6,4},{1,7},{3,1},{5,3},{7,5},{8,14},{10,8},{12,... | collective-permute-start | bytes 245768 | tf_op jit(solution)/shard_map/ppermute | solution.py:498
  60.7 4.4 %main_conv.1 = (bf16[1024,128]{1,0:T(8,128)(2,1)}, bf16[128,1024]{1,0:T(8,128)(2,1)S(1)}, f32[8,1024]{1,0:T(8,128)S(1)}, bf16[32,1024]{1,0:T(8,128)(2,1)S(1)}, b...) custom-call(bf16[1040,128]{1,0:T(8,128)(2,1)S(1)} %payload.1.refs_0_, ...), custom_call_target="tpu_custom_call" | custom-call | flops 40000000 | bytes 120000 | tf_op jit(solution)/shard_map/main_conv/pallas_call | solution.py:36
  65.0 2.3 %collective-permute-done.5.refs_1_ = bf16[64,640]{1,0:T(8,128)(2,1)S(1)} collective-permute-done((bf16[64,640]{1,0:T(8,128)(2,1)S(1)}, bf16[64,640]{1,0:T(8,128)(2,1)S(1)}, u32[]{:S(2)}, u32[]{:S(2)}) %collective-permute-start.5) | collective-permute-done | bytes 81952 | tf_op jit(solution)/shard_map/ppermute | solution.py:498
  67.3 0.1 collective-permute-done.6.refs_2_
  67.4 0.2 collective-permute-done.7.refs_3_
  67.6 0.4 dispatch.1
  68.0 16.9 %all_to_all.5.mine_ref = bf16[32,8,512]{2,1,0:T(8,128)(2,1)S(1)} all-to-all(bf16[32,8,512]{2,1,0:T(8,128)(2,1)S(1)} %dispatch.1), channel_id=1, replica_groups=mesh['dp'=32,'zh'=4,'c'=2] {'dp'}, dimensions={0} | all-to-all | bytes 524288 | tf_op jit(solution)/shard_map/all_to_all | solution.py:540
  85.0 3.3 %collective-permute-start.18 = (bf16[32,1024]{1,0:T(8,128)(2,1)S(1)}, bf16[32,1024]{1,0:T(8,128)(2,1)S(1)}, u32[]{:S(2)}, u32[]{:S(2)}) collective-permute-start(bf16[32,1024]{1,0:T(8,128)(2,1)S(1)} %get-tuple-element.43.tail_ref), channel_id=1, source_target_pairs={{0,8},{8,16},{16,24},{24,32},{32,40},{40,48},{48,56},{56,64},{64,7... | collective-permute-start | bytes 196616 | tf_op jit(solution)/shard_map/ppermute | solution.py:536
  88.3 5.5 %collective-permute-start.19 = (bf16[16,1024]{1,0:T(8,128)(2,1)S(1)}, bf16[16,1024]{1,0:T(8,128)(2,1)S(1)}, u32[]{:S(2)}, u32[]{:S(2)}) collective-permute-start(bf16[16,1024]{1,0:T(8,128)(2,1)S(1)} %slice.11), channel_id=1, source_target_pairs={{8,0},{16,8},{24,16},{32,24},{40,32},{48,40},{56,48},{64,56},{72,6... | collective-permute-start | bytes 98312 | tf_op jit(solution)/shard_map/ppermute | solution.py:537
  93.8 0.7 copy.20
  94.5 0.9 collective-permute-done.19.after_ref
  95.4 2.0 %final_conv.1 = bf16[1024,128]{1,0:T(8,128)(2,1)} custom-call(bf16[32,8,512]{2,1,0:T(8,128)(2,1)S(1)} %all_to_all.5.mine_ref, bf16[32,8,512]{2,1,0:T(8,128)(2,1)S(1)} %collective-permute-done.17.peer_ref, bf16[128,1024]{1,0:T(8,128)(2,1)S(1)} %get-tuple-element.45.raw_ref, ...), custom_call_target="tpu_custom_call", output_to_operand_aliasing={{}: (11, {})} | custom-call | flops 30000000 | bytes 90000 | tf_op jit(solution)/shard_map/final_conv/pallas_call | solution.py:36
  (22 shorter events, 0.3 us)
Async XLA Ops:
  9.3 8.7 %collective-permute-start = (bf16[4,64,1024]{2,1,0:T(8,128)(2,1)S(1)}, bf16[4,64,1024]{2,1,0:T(8,128)(2,1)S(1)}, u32[]{:S(2)}, u32[]{:S(2)}) collective-permute-start(bf16[4,64,1024]{2,1,0:T(8,128)(2,1)S(1)} %get-tuple-element.31), channel_id=1, source_target_pairs={{0,1},{1,0},{2,3},{3,2},{4,5},{5,4},{6,7},{7,6},{8,9},{9,8},{10,11... | collective-permute-start | bytes 1572872 | tf_op jit(solution)/shard_map/ppermute | solution.py:502
  9.4 34.6 %collective-permute-start.9 = (bf16[1040,128]{1,0:T(8,128)(2,1)S(1)}, bf16[1040,128]{1,0:T(8,128)(2,1)S(1)}, u32[]{:S(2)}, u32[]{:S(2)}) collective-permute-start(bf16[1040,128]{1,0:T(8,128)(2,1)S(1)} %payload.1.refs_0_), channel_id=1, source_target_pairs={{0,6},{2,0},{4,2},{6,4},{1,7},{3,1},{5,3},{7,5},{8,14},{10,8},{12,... | collective-permute-start | bytes 798728 | tf_op jit(solution)/shard_map/ppermute | solution.py:498
  15.8 28.3 %collective-permute-start.11 = (bf16[1040,128]{1,0:T(8,128)(2,1)S(1)}, bf16[1040,128]{1,0:T(8,128)(2,1)S(1)}, u32[]{:S(2)}, u32[]{:S(2)}) collective-permute-start(bf16[1040,128]{1,0:T(8,128)(2,1)S(1)} %payload.1.refs_0_), channel_id=1, source_target_pairs={{0,2},{2,4},{4,6},{6,0},{1,3},{3,5},{5,7},{7,1},{8,10},{10,12},{12... | collective-permute-start | bytes 798728 | tf_op jit(solution)/shard_map/ppermute | solution.py:498
  18.1 16.9 %collective-permute-start.1 = (bf16[64,1024]{1,0:T(8,128)(2,1)S(1)}, bf16[64,1024]{1,0:T(8,128)(2,1)S(1)}, u32[]{:S(2)}, u32[]{:S(2)}) collective-permute-start(bf16[64,1024]{1,0:T(8,128)(2,1)S(1)} %get-tuple-element.32), channel_id=1, source_target_pairs={{0,4},{2,6},{4,0},{6,2},{1,5},{3,7},{5,1},{7,3},{8,12},{10,14},{12... | collective-permute-start | bytes 393224 | tf_op jit(solution)/shard_map/ppermute | solution.py:498
  22.0 20.9 %collective-permute-start.2 = (bf16[64,1024]{1,0:T(8,128)(2,1)S(1)}, bf16[64,1024]{1,0:T(8,128)(2,1)S(1)}, u32[]{:S(2)}, u32[]{:S(2)}) collective-permute-start(bf16[64,1024]{1,0:T(8,128)(2,1)S(1)} %get-tuple-element.33), channel_id=1, source_target_pairs={{0,2},{2,4},{4,6},{6,0},{1,3},{3,5},{5,7},{7,1},{8,10},{10,12},{12... | collective-permute-start | bytes 393224 | tf_op jit(solution)/shard_map/ppermute | solution.py:498
  24.6 18.2 %collective-permute-start.3 = (bf16[64,1024]{1,0:T(8,128)(2,1)S(1)}, bf16[64,1024]{1,0:T(8,128)(2,1)S(1)}, u32[]{:S(2)}, u32[]{:S(2)}) collective-permute-start(bf16[64,1024]{1,0:T(8,128)(2,1)S(1)} %get-tuple-element.34), channel_id=1, source_target_pairs={{0,6},{2,0},{4,2},{6,4},{1,7},{3,1},{5,3},{7,5},{8,14},{10,8},{12,... | collective-permute-start | bytes 393224 | tf_op jit(solution)/shard_map/ppermute | solution.py:498
  43.4 1.9 %collective-permute-start.4 = (bf16[64,640]{1,0:T(8,128)(2,1)S(1)}, bf16[64,640]{1,0:T(8,128)(2,1)S(1)}, u32[]{:S(2)}, u32[]{:S(2)}) collective-permute-start(bf16[64,640]{1,0:T(8,128)(2,1)S(1)} %get-tuple-element.39), channel_id=1, source_target_pairs={{0,1},{1,0},{2,3},{3,2},{4,5},{5,4},{6,7},{7,6},{8,9},{9,8},{10,11... | collective-permute-start | bytes 245768 | tf_op jit(solution)/shard_map/ppermute | solution.py:502
  43.5 12.2 %collective-permute-start.8 = (bf16[1040,128]{1,0:T(8,128)(2,1)S(1)}, bf16[1040,128]{1,0:T(8,128)(2,1)S(1)}, u32[]{:S(2)}, u32[]{:S(2)}) collective-permute-start(bf16[1040,128]{1,0:T(8,128)(2,1)S(1)} %payload.1.refs_0_), channel_id=1, source_target_pairs={{0,1},{1,0},{2,3},{3,2},{4,5},{5,4},{6,7},{7,6},{8,9},{9,8},{10,11... | collective-permute-start | bytes 798728 | tf_op jit(solution)/shard_map/ppermute | solution.py:502
  44.0 12.0 %collective-permute-start.10 = (bf16[1040,128]{1,0:T(8,128)(2,1)S(1)}, bf16[1040,128]{1,0:T(8,128)(2,1)S(1)}, u32[]{:S(2)}, u32[]{:S(2)}) collective-permute-start(bf16[1040,128]{1,0:T(8,128)(2,1)S(1)} %collective-permute-done.9.refs_2_), channel_id=1, source_target_pairs={{0,1},{1,0},{2,3},{3,2},{4,5},{5,4},{6,7},{7,6},{8,9},{9,8},{10,11... | collective-permute-start | bytes 798728 | tf_op jit(solution)/shard_map/ppermute | solution.py:502
  44.1 15.1 %collective-permute-start.16 = (bf16[1040,128]{1,0:T(8,128)(2,1)S(1)}, bf16[1040,128]{1,0:T(8,128)(2,1)S(1)}, u32[]{:S(2)}, u32[]{:S(2)}) collective-permute-start(bf16[1040,128]{1,0:T(8,128)(2,1)S(1)} %collective-permute-done.11.refs_8_), channel_id=1, source_target_pairs={{0,1},{1,0},{2,3},{3,2},{4,5},{5,4},{6,7},{7,6},{8,9},{9,8},{10,11... | collective-permute-start | bytes 798728 | tf_op jit(solution)/shard_map/ppermute | solution.py:502
  44.5 9.5 %collective-permute-start.14 = (bf16[528,128]{1,0:T(8,128)(2,1)S(1)}, bf16[528,128]{1,0:T(8,128)(2,1)S(1)}, u32[]{:S(2)}, u32[]{:S(2)}) collective-permute-start(bf16[528,128]{1,0:T(8,128)(2,1)S(1)} %slice.13), channel_id=1, source_target_pairs={{0,6},{2,0},{4,2},{6,4},{1,7},{3,1},{5,3},{7,5},{8,14},{10,8},{12,... | collective-permute-start | bytes 405512 | tf_op jit(solution)/shard_map/ppermute | solution.py:498
  45.3 10.2 %collective-permute-start.12 = (bf16[512,128]{1,0:T(8,128)(2,1)S(1)}, bf16[512,128]{1,0:T(8,128)(2,1)S(1)}, u32[]{:S(2)}, u32[]{:S(2)}) collective-permute-start(bf16[512,128]{1,0:T(8,128)(2,1)S(1)} %slice.12), channel_id=1, source_target_pairs={{0,2},{2,4},{4,6},{6,0},{1,3},{3,5},{5,7},{7,1},{8,10},{10,12},{12... | collective-permute-start | bytes 393224 | tf_op jit(solution)/shard_map/ppermute | solution.py:498
  54.0 6.7 %collective-permute-start.15 = (bf16[528,128]{1,0:T(8,128)(2,1)S(1)}, bf16[528,128]{1,0:T(8,128)(2,1)S(1)}, u32[]{:S(2)}, u32[]{:S(2)}) collective-permute-start(bf16[528,128]{1,0:T(8,128)(2,1)S(1)} %collective-permute-done.14.refs_6_), channel_id=1, source_target_pairs={{0,1},{1,0},{2,3},{3,2},{4,5},{5,4},{6,7},{7,6},{8,9},{9,8},{10,11... | collective-permute-start | bytes 405512 | tf_op jit(solution)/shard_map/ppermute | solution.py:502
  55.5 5.2 %collective-permute-start.13 = (bf16[512,128]{1,0:T(8,128)(2,1)S(1)}, bf16[512,128]{1,0:T(8,128)(2,1)S(1)}, u32[]{:S(2)}, u32[]{:S(2)}) collective-permute-start(bf16[512,128]{1,0:T(8,128)(2,1)S(1)} %collective-permute-done.12.refs_4_), channel_id=1, source_target_pairs={{0,1},{1,0},{2,3},{3,2},{4,5},{5,4},{6,7},{7,6},{8,9},{9,8},{10,11... | collective-permute-start | bytes 393224 | tf_op jit(solution)/shard_map/ppermute | solution.py:502
  55.7 11.6 %collective-permute-start.5 = (bf16[64,640]{1,0:T(8,128)(2,1)S(1)}, bf16[64,640]{1,0:T(8,128)(2,1)S(1)}, u32[]{:S(2)}, u32[]{:S(2)}) collective-permute-start(bf16[64,640]{1,0:T(8,128)(2,1)S(1)} %join.1.refs_0_), channel_id=1, source_target_pairs={{0,4},{2,6},{4,0},{6,2},{1,5},{3,7},{5,1},{7,3},{8,12},{10,14},{12... | collective-permute-start | bytes 245768 | tf_op jit(solution)/shard_map/ppermute | solution.py:498
  56.0 11.5 %collective-permute-start.6 = (bf16[64,640]{1,0:T(8,128)(2,1)S(1)}, bf16[64,640]{1,0:T(8,128)(2,1)S(1)}, u32[]{:S(2)}, u32[]{:S(2)}) collective-permute-start(bf16[64,640]{1,0:T(8,128)(2,1)S(1)} %join.1.refs_0_), channel_id=1, source_target_pairs={{0,2},{2,4},{4,6},{6,0},{1,3},{3,5},{5,7},{7,1},{8,10},{10,12},{12... | collective-permute-start | bytes 245768 | tf_op jit(solution)/shard_map/ppermute | solution.py:498
  59.2 8.4 %collective-permute-start.7 = (bf16[64,640]{1,0:T(8,128)(2,1)S(1)}, bf16[64,640]{1,0:T(8,128)(2,1)S(1)}, u32[]{:S(2)}, u32[]{:S(2)}) collective-permute-start(bf16[64,640]{1,0:T(8,128)(2,1)S(1)} %join.1.refs_0_), channel_id=1, source_target_pairs={{0,6},{2,0},{4,2},{6,4},{1,7},{3,1},{5,3},{7,5},{8,14},{10,8},{12,... | collective-permute-start | bytes 245768 | tf_op jit(solution)/shard_map/ppermute | solution.py:498
  85.0 10.5 %collective-permute-start.17 = (bf16[32,8,512]{2,1,0:T(8,128)(2,1)S(1)}, bf16[32,8,512]{2,1,0:T(8,128)(2,1)S(1)}, u32[]{:S(2)}, u32[]{:S(2)}) collective-permute-start(bf16[32,8,512]{2,1,0:T(8,128)(2,1)S(1)} %all_to_all.5.mine_ref), channel_id=1, source_target_pairs={{0,1},{1,0},{2,3},{3,2},{4,5},{5,4},{6,7},{7,6},{8,9},{9,8},{10,11... | collective-permute-start | bytes 786440 | tf_op jit(solution)/shard_map/ppermute | solution.py:502
  85.0 10.4 %collective-permute-start.18 = (bf16[32,1024]{1,0:T(8,128)(2,1)S(1)}, bf16[32,1024]{1,0:T(8,128)(2,1)S(1)}, u32[]{:S(2)}, u32[]{:S(2)}) collective-permute-start(bf16[32,1024]{1,0:T(8,128)(2,1)S(1)} %get-tuple-element.43.tail_ref), channel_id=1, source_target_pairs={{0,8},{8,16},{16,24},{24,32},{32,40},{40,48},{48,56},{56,64},{64,7... | collective-permute-start | bytes 196616 | tf_op jit(solution)/shard_map/ppermute | solution.py:536
  88.3 7.1 %collective-permute-start.19 = (bf16[16,1024]{1,0:T(8,128)(2,1)S(1)}, bf16[16,1024]{1,0:T(8,128)(2,1)S(1)}, u32[]{:S(2)}, u32[]{:S(2)}) collective-permute-start(bf16[16,1024]{1,0:T(8,128)(2,1)S(1)} %slice.11), channel_id=1, source_target_pairs={{8,0},{16,8},{24,16},{32,24},{40,32},{48,40},{56,48},{64,56},{72,6... | collective-permute-start | bytes 98312 | tf_op jit(solution)/shard_map/ppermute | solution.py:537

commit v2 on v1

--- a/solution.py
+++ b/solution.py
@@ -15,6 +15,9 @@
 F32 = jnp.float32
 BF16 = jnp.bfloat16
 ORDER = (2, 1, 3, 0)
+HEAD = 32 * CAP
+EDGE = 16
+TOP = HEAD + EDGE
 VM = pl.BlockSpec(memory_space=pltpu.VMEM)
 ANY = pl.BlockSpec(memory_space=pl.ANY)
 DMA = pltpu.SemaphoreType.DMA
@@ -227,58 +230,98 @@
     return call(pair_kernel, "pair", [pltpu.VMEM((rows, width), BF16)] * (ZH - 1), (own, peer), cost=work(0.5))
 
 
-def split_sum(total):
-    hi = total.astype(BF16).astype(F32)
-    lo = total - hi
-    lane = iota((total.shape[0], 128), 1)
-    return jnp.where(lane == 0, hi, jnp.where(lane == 1, lo, 0.0)).astype(BF16)
-
-
-def hidden_kernel(own_ref, peer_ref, r2_ref, r1_ref, r3_ref, gain_ref, codec_ref, hid_ref, keep_ref, send_ref):
+def squares_row(total):
+    rows = total.shape[0]
+    diag = iota((rows, 128), 0) == iota((rows, 128), 1)
+    line = jnp.sum(jnp.where(diag, jnp.broadcast_to(total, (rows, 128)), 0.0), axis=0, keepdims=True)
+    hi = line.astype(BF16).astype(F32)
+    return hi, line - hi
+
+
+def squares_column(line, rows):
+    diag = iota((rows, 128), 0) == iota((rows, 128), 1)
+    return jnp.sum(jnp.where(diag, jnp.broadcast_to(line, (rows, 128)), 0.0), axis=1, keepdims=True)
+
+
+def with_squares(block, hi, lo):
+    row = iota(block.shape, 0)
+    return jnp.where(row == 0, hi, jnp.where(row == 1, lo, block))
+
+
+def hidden_kernel(
+    own_ref, peer_ref, r2_ref, r1_ref, r3_ref, gain_ref, codec_ref, before_ref, after_ref, hid_hbm, keep_ref, send_ref, total_ref, hid_ref, sem
+):
     half = codec_ref.shape[1] // 2
+    width = codec_ref.shape[0]
     last = ORDER.index(0)
     total = own_ref[last] + peer_ref[last].astype(F32)
     total = total + r2_ref[...].astype(F32) + (r1_ref[...].astype(F32) + r3_ref[...].astype(F32))
     hidden = total.astype(BF16)
     hid_ref[...] = hidden
+    copy = pltpu.make_async_copy(hid_ref, hid_hbm, sem)
+    copy.start()
     wide = hidden.astype(F32)
     normed = (wide * gain_ref[...]).astype(BF16)
     squares = jnp.sum(wide * wide, axis=1, keepdims=True)
     part = jnp.dot(normed, codec_ref[...], preferred_element_type=F32)
     left, right = part[:, :half], part[:, half:]
     first = lax.axis_index("c") == 0
-    keep_ref[:, :half] = jnp.where(first, left, right)
+    keep_ref[...] = jnp.where(first, left, right)
     send_ref[:, :half] = jnp.where(first, right, left).astype(BF16)
-    keep_ref[:, half:] = jnp.broadcast_to(squares, (squares.shape[0], 128))
-    send_ref[:, half:] = split_sum(squares)
-
-
-def hidden_step(own, peer, r2, r1, r3, gain, codec):
+    total_ref[...] = squares
+    hi, lo = squares_row(squares)
+    send_ref[0:EDGE, half:] = with_squares(before_ref[...].astype(F32), hi, lo).astype(BF16)
+    send_ref[EDGE : 2 * EDGE, half:] = after_ref[...]
+    send_ref[2 * EDGE :, half:] = jnp.zeros((send_ref.shape[0] - 2 * EDGE, 128), BF16)
+    copy.wait()
+
+
+def hidden_step(own, peer, r2, r1, r3, gain, codec, before, after):
     rows, width = r2.shape
-    ext = codec.shape[1] // 2 + 128
-    outs = [pltpu.VMEM((rows, width), BF16), pltpu.VMEM((rows, ext), F32), pltpu.VMEM((rows, ext), BF16)]
-    return call(hidden_kernel, "hidden", outs, (own, peer, r2, r1, r3, gain, codec), cost=work(2))
-
-
-def join_kernel(keep_ref, recv_ref, out_ref):
-    half = keep_ref.shape[1] - 128
-    recv = recv_ref[...].astype(F32)
-    out_ref[:, :half] = (keep_ref[:, :half] + recv[:, :half]).astype(BF16)
-    squares = keep_ref[:, half : half + 1] + recv[:, half : half + 1] + recv[:, half + 1 : half + 2]
-    out_ref[:, half:] = split_sum(squares)
-
-
-def join(keep, recv):
-    return call(join_kernel, "join", pltpu.VMEM(recv.shape, BF16), (keep, recv), cost=work(0.3))
+    half = codec.shape[1] // 2
+    outs = [
+        pltpu.HBM((rows, width), BF16),
+        pltpu.VMEM((rows, half), F32),
+        pltpu.VMEM((rows, half + 128), BF16),
+        pltpu.VMEM((rows, 1), F32),
+    ]
+    ins = (own, peer, r2, r1, r3, gain, codec, before, after)
+    return call(hidden_kernel, "hidden", outs, ins, [pltpu.VMEM((rows, width), BF16), DMA], far_outs=(0,), cost=work(2))
+
+
+def join_kernel(keep_ref, total_ref, recv_ref, before_ref, after_ref, out_ref):
+    half = keep_ref.shape[1]
+    first = lax.axis_index("c") == 0
+    out_ref[:, :half] = (keep_ref[...] + recv_ref[:, :half].astype(F32)).astype(BF16)
+    mate = recv_ref[:, half:].astype(F32)
+    line = mate[0:1] + mate[1:2]
+    mine_hi, mine_lo = squares_row(total_ref[...])
+    line = line + (mine_hi + mine_lo)
+    hi = line.astype(BF16).astype(F32)
+    for at, own, other in ((0, before_ref, mate[0:EDGE]), (2 * EDGE, after_ref, mate[EDGE : 2 * EDGE])):
+        own = own[...].astype(F32)
+        low = jnp.where(first, own, other)
+        if at == 0:
+            low = with_squares(low, hi, line - hi)
+        out_ref[at : at + EDGE, half:] = low.astype(BF16)
+        out_ref[at + EDGE : at + 2 * EDGE, half:] = jnp.where(first, other, own).astype(BF16)
+
+
+def join(keep, total, recv, before, after):
+    return call(join_kernel, "join", pltpu.VMEM(recv.shape, BF16), (keep, total, recv, before, after), cost=work(0.3))
 
 
 def dispatch_kernel(features, a_ref, b_ref, c_ref, d_ref, tgt_ref, out_ref):
     half = a_ref.shape[1] - 128
     owners, slots, _ = out_ref.shape
     rows = a_ref.shape[0]
-    total = (a_ref[...].astype(F32) + b_ref[...].astype(F32)) + (c_ref[...].astype(F32) + d_ref[...].astype(F32))
-    squares = total[:, half : half + 1] + total[:, half + 1 : half + 2]
-    latent = (total[:, :half] * lax.rsqrt(squares / features + 1e-05)).astype(BF16)
+    parts = (a_ref, b_ref, c_ref, d_ref)
+    a, b, c, d = (p[:, :half].astype(F32) for p in parts)
+    a2, b2, c2, d2 = (p[0:EDGE, half:].astype(F32) for p in parts)
+    total = (a + b) + (c + d)
+    lines = (a2 + b2) + (c2 + d2)
+    squares = squares_column(lines[0:1] + lines[1:2], rows)
+    latent = (total * lax.rsqrt(squares / features + 1e-05)).astype(BF16)
     place = iota((owners * slots, rows), 0)
     onehot = ((place == tgt_ref[0:1]) | (place == tgt_ref[1:2])).astype(F32).astype(BF16)
     placed = jnp.dot(onehot, latent, preferred_element_type=F32)
@@ -291,47 +334,59 @@
     return call(kernel, "dispatch", pltpu.VMEM((owners, 2 * CAP, half), BF16), (*parts, targets), cost=work(1))
 
 
-def payload_kernel(frames_hbm, alpha_hbm, out_ref, frames_ref, alpha_ref, sems):
+def payload_kernel(
+    frames_hbm, alpha_hbm, filt_hbm, bias_hbm, out_ref, head_ref, tail_ref, frames_ref, wcat_ref, bias_ref, alpha_ref, sems
+):
     copies = [
         pltpu.make_async_copy(alpha_hbm, alpha_ref, sems.at[0]),
         pltpu.make_async_copy(frames_hbm, frames_ref, sems.at[1]),
+        pltpu.make_async_copy(bias_hbm, bias_ref, sems.at[2]),
     ]
+    width = frames_ref.shape[1]
+    for t in range(TAPS):
+        copies.append(pltpu.make_async_copy(filt_hbm.at[t], wcat_ref.at[:, pl.ds(t * width, width)], sems.at[3 + t]))
     for copy in copies:
         copy.start()
-    for copy in copies:
+    for copy in copies[:2]:
         copy.wait()
-    count, width = frames_ref.shape
+    count = frames_ref.shape[0]
     first = out_ref.shape[0] - count
     raw = frames_ref[...]
-    early = 32 * CAP
     alpha = alpha_ref[...]
-    mix = raw[early:].astype(F32)
+    mix = raw[HEAD:].astype(F32)
     act = mix + sin_squared(alpha * mix) * (1.0 / alpha)
-    out_ref[0:early] = raw[:early]
-    out_ref[early:count] = act.astype(BF16)
+    out_ref[0:HEAD] = raw[:HEAD]
+    out_ref[HEAD:count] = act.astype(BF16)
+    head_ref[...] = raw[:EDGE]
+    tail_ref[...] = act[count - HEAD - EDGE :].astype(BF16)
     hi = alpha.astype(BF16).astype(F32)
     mid = (alpha - hi).astype(BF16).astype(F32)
     lo = alpha - hi - mid
     row = iota((first, width), 0)
     out_ref[count:] = jnp.where(row == 0, hi, jnp.where(row == 1, mid, jnp.where(row == 2, lo, 0.0))).astype(BF16)
-
-
-def payload(frames, alpha):
+    for copy in copies[2:]:
+        copy.wait()
+
+
+def payload(frames, alpha, filt, bias):
     count, width = frames.shape
+    channels = filt.shape[1]
     return call(
         payload_kernel,
         "payload",
-        pltpu.VMEM((count + 16, width), BF16),
-        (frames, alpha.reshape(1, width)),
-        scratch=[pltpu.VMEM((count, width), BF16), pltpu.VMEM((1, width), F32), DMA((2,))],
-        far=(0, 1),
-        cost=work(1.5),
+        [
+            pltpu.VMEM((count + 16, width), BF16),
+            pltpu.VMEM((EDGE, width), BF16),
+            pltpu.VMEM((EDGE, width), BF16),
+            pltpu.VMEM((count, width), BF16),
+            pltpu.VMEM((channels, TAPS * width), BF16),
+            pltpu.VMEM((1, width), F32),
+        ],
+        (frames, alpha.reshape(1, width), filt, bias.reshape(1, width)),
+        scratch=[pltpu.VMEM((1, width), F32), DMA((3 + TAPS,))],
+        far=(0, 1, 2, 3),
+        cost=work(2),
     )
-
-
-HEAD = 32 * CAP
-EDGE = 16
-TOP = HEAD + EDGE
 
 
 def taps_sum(y, base, count):
@@ -343,80 +398,54 @@
     return total
 
 
-CUT = 512
-
-
 def main_kernel(*refs):
-    pieces = refs[:10]
-    filt_hbm, own_hbm, bias_hbm, audio_hbm, raw_ref, alpha_ref, near_ref, tail_ref, wcat_ref, ends_ref, bias_ref = refs[10:21]
-    act_ref, y_ref, own_ref, out_ref, sems = refs[21:]
+    pieces = refs[:8]
+    wcat_ref, own_ref, bias_ref, audio_hbm, raw_ref, alpha_ref, near_ref, tail_ref = refs[8:16]
+    act_ref, y_ref, out_ref, sem = refs[16:]
     chip, core = lax.axis_index("zh"), lax.axis_index("c")
-    copies = [
-        pltpu.make_async_copy(filt_hbm.at[t], wcat_ref.at[:, pl.ds(t * 128, 128)], sems.at[t]) for t in range(TAPS)
-    ]
-    copies.append(pltpu.make_async_copy(own_hbm, own_ref, sems.at[TAPS]))
-    copies.append(pltpu.make_async_copy(bias_hbm, bias_ref, sems.at[TAPS + 1]))
-    for copy in copies:
-        copy.start()
     count = own_ref.shape[0]
     for k in range(8):
         source = lax.rem(chip + k // 2, ZH) * 2 + (core if k % 2 == 0 else 1 - core)
         cols = pl.ds(pl.multiple_of(source * 128, 128), 128)
-        if k // 2 == 2:
-            head, rest = pieces[4 + k % 2], pieces[6 + k % 2]
-            act_ref[0 : CUT - HEAD, cols] = head[HEAD:CUT]
-            act_ref[CUT - HEAD :, cols] = rest[0 : count - CUT]
-            extra = rest[count - CUT :]
-        else:
-            head = pieces[k if k < 4 else k + 2]
-            act_ref[:, cols] = head[HEAD:count]
-            extra = head[count : count + 16]
+        head = pieces[k]
+        act_ref[:, cols] = head[HEAD:count]
         raw_ref[:, cols] = head[0:HEAD]
-        extra = extra.astype(F32)
+        extra = head[count : count + 16].astype(F32)
         alpha_ref[:, cols] = jnp.broadcast_to(extra[0:1] + extra[1:2] + extra[2:3], (8, 128))
     near_ref[...] = act_ref[0 : 2 * EDGE]
     tail_ref[...] = act_ref[count - HEAD - 2 * EDGE : count - HEAD]
-    for copy in copies:
-        copy.wait()
     y_ref[...] = jnp.dot(act_ref[...], wcat_ref[...], preferred_element_type=F32)
     inner = count - TOP - EDGE
     conv = taps_sum(y_ref, EDGE, inner)
     mix = own_ref[TOP : TOP + inner].astype(F32)
     out_ref[...] = (mix + bias_ref[...] + conv).astype(BF16)
-    ends_ref[0:TOP] = own_ref[0:TOP]
-    ends_ref[TOP:] = own_ref[count - EDGE : count]
-    last = pltpu.make_async_copy(out_ref, audio_hbm.at[pl.ds(TOP, inner)], sems.at[TAPS + 2])
+    last = pltpu.make_async_copy(out_ref, audio_hbm.at[pl.ds(TOP, inner)], sem)
     last.start()
     last.wait()
 
 
-def main_conv(pieces, filt, frames, bias):
-    count, width = frames.shape
-    taps, channels, _ = filt.shape
+def main_conv(pieces, wcat, own, bias):
+    count, width = own.shape
+    channels = wcat.shape[0]
     outs = [
         pltpu.HBM((count, width), BF16),
         pltpu.VMEM((HEAD, channels), BF16),
         pltpu.VMEM((8, channels), F32),
         pltpu.VMEM((2 * EDGE, channels), BF16),
         pltpu.VMEM((2 * EDGE, channels), BF16),
-        pltpu.VMEM((channels, taps * width), BF16),
-        pltpu.VMEM((TOP + EDGE, width), BF16),
-        pltpu.VMEM((1, width), F32),
     ]
     scratch = [
         pltpu.VMEM((count - HEAD, channels), BF16),
-        pltpu.VMEM((count - HEAD, taps * width), F32),
-        pltpu.VMEM((count, width), BF16),
+        pltpu.VMEM((count - HEAD, TAPS * width), F32),
         pltpu.VMEM((count - TOP - EDGE, width), BF16),
-        DMA((TAPS + 3,)),
+        DMA,
     ]
-    ins = (*pieces, filt, frames, bias.reshape(1, width))
-    return call(main_kernel, "main_conv", outs, ins, scratch, far=(10, 11, 12), far_outs=(0,), mib=16, cost=work(4))
+    return call(main_kernel, "main_conv", outs, (*pieces, wcat, own, bias), scratch, far_outs=(0,), mib=16, cost=work(4))
 
 
 def final_kernel(
-    mine_ref, peer_ref, raw_ref, alpha_ref, near_ref, tail_ref, before_ref, after_ref, wcat_ref, ends_ref, bias_ref, audio_ref,
-    out_ref, act_ref, y_ref, out_top_ref, out_low_ref, top_sem, low_sem,
+    mine_ref, peer_ref, raw_ref, alpha_ref, near_ref, tail_ref, p0_ref, p1_ref, p2_ref, p3_ref, wcat_ref, ends_ref, bias_ref, audio_ref,
+    out_ref, act_ref, after_ref, y_ref, out_top_ref, out_low_ref, top_sem, low_sem,
 ):
     del audio_ref
     core, chip = lax.axis_index("c"), lax.axis_index("zh")
@@ -436,6 +465,11 @@
     pick = (place == jnp.where(row < HEAD, own_place, after_place)).astype(F32).astype(BF16)
     alpha = alpha_ref[0:1]
     inv = 1.0 / alpha
+    for d, part in enumerate((p0_ref, p1_ref, p2_ref, p3_ref)):
+        for k in range(2):
+            cols = pl.ds(pl.multiple_of((lax.rem(chip + ZH - d, ZH) * 2 + k) * 128, 128), 128)
+            act_ref[0:EDGE, cols] = part[k * EDGE : (k + 1) * EDGE, half:]
+            after_ref[:, cols] = part[(2 + k) * EDGE : (3 + k) * EDGE, half:]
     taken = []
     for k, side in ((0, left), (1, right)):
         cols = slice(k * half, (k + 1) * half)
@@ -445,7 +479,6 @@
         act_ref[EDGE : EDGE + HEAD, cols] = (mix + sin_squared(alpha[:, cols] * mix) * inv[:, cols]).astype(BF16)
         mix = after_ref[:, cols].astype(F32) + got[HEAD:]
         act_ref[EDGE + HEAD + 4 * EDGE :, cols] = (mix + sin_squared(alpha[:, cols] * mix) * inv[:, cols]).astype(BF16)
-    act_ref[0:EDGE] = before_ref[EDGE:]
     act_ref[EDGE + HEAD : EDGE + HEAD + 2 * EDGE] = near_ref[...]
     act_ref[EDGE + HEAD + 2 * EDGE : EDGE + HEAD + 4 * EDGE] = tail_ref[...]
     y_ref[...] = jnp.dot(act_ref[...], wcat_ref[...], preferred_element_type=F32)
@@ -460,7 +493,7 @@
     out_top_ref[0:HEAD] = (mix[:HEAD] + got + bias + conv[:HEAD]).astype(BF16)
     out_top_ref[HEAD:] = (mix[HEAD:] + bias + conv[HEAD:]).astype(BF16)
     conv = taps_sum(y_ref, EDGE + HEAD + 3 * EDGE, EDGE)
-    out_low_ref[...] = (ends_ref[TOP:].astype(F32) + bias + conv).astype(BF16)
+    out_low_ref[...] = (ends_ref[count - EDGE : count].astype(F32) + bias + conv).astype(BF16)
     top_copy = pltpu.make_async_copy(out_top_ref, out_ref.at[0:TOP], top_sem)
     low_copy = pltpu.make_async_copy(out_low_ref, out_ref.at[count - EDGE : count], low_sem)
     top_copy.start()
@@ -469,7 +502,7 @@
     low_copy.wait()
 
 
-def final_conv(mine, peer, raw, alpha, near, tail, before, after, wcat, ends, bias, audio):
+def final_conv(mine, peer, raw, alpha, near, tail, parts, wcat, ends, bias, audio):
     count, width = audio.shape
     channels = raw.shape[1]
     stack = EDGE + HEAD + 5 * EDGE
@@ -477,19 +510,20 @@
         final_kernel,
         "final_conv",
         pltpu.HBM((count, width), BF16),
-        (mine, peer, raw, alpha, near, tail, before, after, wcat, ends, bias, audio),
+        (mine, peer, raw, alpha, near, tail, *parts, wcat, ends, bias, audio),
         scratch=[
             pltpu.VMEM((stack, channels), BF16),
+            pltpu.VMEM((EDGE, channels), BF16),
             pltpu.VMEM((stack, TAPS * width), F32),
             pltpu.VMEM((TOP, width), BF16),
             pltpu.VMEM((EDGE, width), BF16),
             DMA,
             DMA,
         ],
-        far=(11,),
+        far=(13,),
         far_outs=(0,),
         mib=16,
-        alias={11: 0},
+        alias={13: 0},
         cost=work(3),
     )
 
@@ -513,33 +547,33 @@
     owners = lax.axis_size("dp")
     width = norm_gain.shape[0]
 
-    sent = payload(frames, snake_alpha)
-    left, right = rotate(sent, 1), rotate(sent, 3)
+    sent, head, tail, mine, wcat, bias = payload(frames, snake_alpha, filter_weight, conv_bias)
+    left = rotate(sent, 1)
+    right = rotate(sent, 3)
+    before = lax.ppermute(tail, "dp", [(i, i + 1) for i in range(owners - 1)])
+    after = lax.ppermute(head, "dp", [(i + 1, i) for i in range(owners - 1)])
     query = after_all(query, sent)
     theirs, attended, weight, targets = attend(
         query, new_key, new_value, cache_key, cache_value, cache_len, finished, owner, out_weight, width
     )
+    theirs = after_all(theirs, left, right, before, after)
     peer = swap(theirs)
     own, codec, gain = project(attended, weight, residual, codec_weight, norm_gain)
-    got = {d: rotate(x, d) for d, x in zip(ORDER, pair(own, peer))}
-    hidden, keep, send = hidden_step(own, peer, got[2], got[1], got[3], gain, codec)
-
-    far_head = rotate(after_all(left[:CUT], hidden), 1)
-    far_rest = rotate(after_all(right[CUT:], hidden), 3)
+    pairs = pair(own, peer)
+    got = {d: rotate(x, d) for d, x in zip(ORDER, pairs)}
+    far = rotate(after_all(right, pairs[0]), 3)
+    hidden, keep, send, total = hidden_step(own, peer, got[2], got[1], got[3], gain, codec, before, after)
+    joined = join(keep, total, swap(send), before, after)
+    parts = [joined] + [rotate(joined, d) for d in (1, 2, 3)]
     pieces = []
-    for x in (sent, right, far_head, far_rest, left):
-        pieces += [x, swap(x)]
-
-    joined = join(keep, swap(send))
-    parts = [joined] + [rotate(joined, d) for d in (2, 1, 3)]
-    audio, raw, alpha, close, tail, wcat, ends, bias = main_conv(pieces, filter_weight, frames, conv_bias)
-    before = lax.ppermute(tail, "dp", [(i, i + 1) for i in range(owners - 1)])
-    after = lax.ppermute(raw[:EDGE], "dp", [(i + 1, i) for i in range(owners - 1)])
-    targets = after_all(targets, tail)
+    for x, when in ((sent, joined), (right, joined), (far, parts[1]), (left, joined)):
+        pieces += [x, swap(after_all(x, when))]
+    audio, raw, alpha, close, low = main_conv(pieces, wcat, mine, bias)
+    targets = after_all(targets, low)
     outgoing = dispatch(residual.shape[1], owners, parts, targets)
     incoming = lax.all_to_all(outgoing, "dp", 0, 0, tiled=True)
     other = swap(incoming)
-    audio = final_conv(incoming, other, raw, alpha, close, tail, before, after, wcat, ends, bias, audio)
+    audio = final_conv(incoming, other, raw, alpha, close, low, parts, wcat, mine, bias, audio)
     return (hidden, audio)
 
 

time: 99.1 us -> 88.6 us (0.89)
  the two profiles are of different devices: /device:TPU:8 before, /device:TPU:1 now
where the time goes in v2:
time: 88.6 us; the launch traced here: 88.4 us
  starting transfers between devices  31.2 us (35%)
  waiting for transfers between devices  22.9 us (26%)
  Pallas kernels  18 us (20%)
  blocking collectives  15.3 us (17%)
  between operations  0.92 us (1%)
    ppermute x9, starting transfers between devices, rotate(): return lax.ppermute(x, 'zh', [(i, (i + d) % ZH) for i in range(ZH)])  21.1 us
    ppermute x9, waiting for transfers between devices, rotate(): return lax.ppermute(x, 'zh', [(i, (i + d) % ZH) for i in range(ZH)])  20.8 us
    pallas_call x9, Pallas kernels, call(): pl.pallas_call(kernel, in_specs=[ANY if i in far else VM for i in range(l...  18 us
    all_to_all x1, blocking collectives, body(): incoming = lax.all_to_all(outgoing, 'dp', 0, 0, tiled=True)  15.3 us
    ppermute x7, starting transfers between devices, swap(): return lax.ppermute(x, 'c', [(0, 1), (1, 0)])  6.25 us
    ppermute x1, starting transfers between devices, body(): before = lax.ppermute(tail, 'dp', [(i, i + 1) for i in range(owners - 1)])  2.63 us
    ppermute x7, waiting for transfers between devices, swap(): return lax.ppermute(x, 'c', [(0, 1), (1, 0)])  2.1 us
  transfers between devices with their start and end apart: 18, of which 10 were waited for; matrix products, arithmetic and copies ran while one was open for 0% of the time, Pallas kernels for 16%

profile of v2, /device:TPU:1, one launch (start us, length us, event | category | flops | bytes accessed | tf_op | source)
XLA Modules:
  0.0 88.4 jit_solution(5975027565885542060)
XLA Ops:
  0.6 1.6 %payload.1 = (bf16[1040,128]{1,0:T(8,128)(2,1)S(1)}, bf16[16,128]{1,0:T(8,128)(2,1)S(1)}, bf16[16,128]{1,0:T(8,128)(2,1)S(1)}, bf16[1024,128]{1,0:T(8,128)(2,1)S...) custom-call(bf16[1024,128]{1,0:T(8,128)(2,1)} %frames_hbm.1, f32[1,128]{1,0:T(1,128)} %bitcast.8, ...), custom_call_target="tpu_custom_call" | custom-call | flops 20000000 | bytes 60000 | tf_op jit(solution)/shard_map/payload/pallas_call | solution.py:39
  2.3 3.9 %collective-permute-start = (bf16[1040,128]{1,0:T(8,128)(2,1)S(1)}, bf16[1040,128]{1,0:T(8,128)(2,1)S(1)}, u32[]{:S(2)}, u32[]{:S(2)}) collective-permute-start(bf16[1040,128]{1,0:T(8,128)(2,1)S(1)} %get-tuple-element.54.refs_0_), channel_id=1, source_target_pairs={{0,2},{2,4},{4,6},{6,0},{1,3},{3,5},{5,7},{7,1},{8,10},{10,12},{12... | collective-permute-start | bytes 798728 | tf_op jit(solution)/shard_map/ppermute | solution.py:532
  6.2 3.1 %collective-permute-start.1 = (bf16[1040,128]{1,0:T(8,128)(2,1)S(1)}, bf16[1040,128]{1,0:T(8,128)(2,1)S(1)}, u32[]{:S(2)}, u32[]{:S(2)}) collective-permute-start(bf16[1040,128]{1,0:T(8,128)(2,1)S(1)} %get-tuple-element.54.refs_0_), channel_id=1, source_target_pairs={{0,6},{2,0},{4,2},{6,4},{1,7},{3,1},{5,3},{7,5},{8,14},{10,8},{12,... | collective-permute-start | bytes 798728 | tf_op jit(solution)/shard_map/ppermute | solution.py:532
  9.3 2.6 %collective-permute-start.2 = (bf16[16,128]{1,0:T(8,128)(2,1)S(1)}, bf16[16,128]{1,0:T(8,128)(2,1)S(1)}, u32[]{:S(2)}, u32[]{:S(2)}) collective-permute-start(bf16[16,128]{1,0:T(8,128)(2,1)S(1)} %get-tuple-element.41), channel_id=1, source_target_pairs={{0,8},{8,16},{16,24},{24,32},{32,40},{40,48},{48,56},{56,64},{64,7... | collective-permute-start | bytes 12296 | tf_op jit(solution)/shard_map/ppermute | solution.py:553
  11.9 1.3 %collective-permute-start.3 = (bf16[16,128]{1,0:T(8,128)(2,1)S(1)}, bf16[16,128]{1,0:T(8,128)(2,1)S(1)}, u32[]{:S(2)}, u32[]{:S(2)}) collective-permute-start(bf16[16,128]{1,0:T(8,128)(2,1)S(1)} %get-tuple-element.42), channel_id=1, source_target_pairs={{8,0},{16,8},{24,16},{32,24},{40,32},{48,40},{56,48},{64,56},{72,6... | collective-permute-start | bytes 12296 | tf_op jit(solution)/shard_map/ppermute | solution.py:554
  13.2 7.3 %attend.1 = (bf16[4,64,1024]{2,1,0:T(8,128)(2,1)S(1)}, bf16[64,512]{1,0:T(8,128)(2,1)S(1)}, bf16[4,512,1024]{2,1,0:T(8,128)(2,1)S(1)}, s32[2,64]{1,0:T(2,128)S(1)}) custom-call(bf16[64,512]{1,0:T(8,128)(2,1)} %q_hbm, bf16[64,512]{1,0:T(8,128)(2,1)} %nk_hbm.1, bf16[64,512]{1,0:T(8,128)(2,1)} %nv_hbm.1, bf16[64,4,16,128]{3,2,1,0:T(8,128)(2,1)} %ck_hbm.1, ...), custom_call_target="tpu_custom_call" | custom-call | flops 60000000 | bytes 180000 | tf_op jit(solution)/shard_map/attend/pallas_call | solution.py:39
  20.5 1.9 %collective-permute-done.1.refs_2_ = bf16[1040,128]{1,0:T(8,128)(2,1)S(1)} collective-permute-done((bf16[1040,128]{1,0:T(8,128)(2,1)S(1)}, bf16[1040,128]{1,0:T(8,128)(2,1)S(1)}, u32[]{:S(2)}, u32[]{:S(2)}) %collective-permute-start.1) | collective-permute-done | bytes 266272 | tf_op jit(solution)/shard_map/ppermute | solution.py:532
  22.4 1.0 %collective-permute-start.4 = (bf16[4,64,1024]{2,1,0:T(8,128)(2,1)S(1)}, bf16[4,64,1024]{2,1,0:T(8,128)(2,1)S(1)}, u32[]{:S(2)}, u32[]{:S(2)}) collective-permute-start(bf16[4,64,1024]{2,1,0:T(8,128)(2,1)S(1)} %get-tuple-element.43), channel_id=1, source_target_pairs={{0,1},{1,0},{2,3},{3,2},{4,5},{5,4},{6,7},{7,6},{8,9},{9,8},{10,11... | collective-permute-start | bytes 1572872 | tf_op jit(solution)/shard_map/ppermute | solution.py:536
  23.4 2.2 %project.1 = (f32[4,64,1024]{2,1,0:T(8,128)S(1)}, bf16[1024,1024]{1,0:T(8,128)(2,1)S(1)}, f32[1,1024]{1,0:T(1,128)S(1)}) custom-call(bf16[64,512]{1,0:T(8,128)(2,1)S(1)} %get-tuple-element.37.att_ref, bf16[4,512,1024]{2,1,0:T(8,128)(2,1)S(1)} %get-tuple-element.38.w_ref, bf16[64,8192]{1,0:T(8,128)(2,1)} %res_hbm.1, bf16[1024,1024]{1,0:T(8,128)(2,1)} %codec_hbm.1, ...), custom_call_target="tpu_custom_call" | custom-call | flops 20000000 | bytes 60000 | tf_op jit(solution)/shard_map/project/pallas_call | solution.py:39
  25.7 3.7 %collective-permute-start.5 = (bf16[64,1024]{1,0:T(8,128)(2,1)S(1)}, bf16[64,1024]{1,0:T(8,128)(2,1)S(1)}, u32[]{:S(2)}, u32[]{:S(2)}) collective-permute-start(bf16[64,1024]{1,0:T(8,128)(2,1)S(1)} %get-tuple-element.44), channel_id=1, source_target_pairs={{0,4},{2,6},{4,0},{6,2},{1,5},{3,7},{5,1},{7,3},{8,12},{10,14},{12... | collective-permute-start | bytes 393224 | tf_op jit(solution)/shard_map/ppermute | solution.py:532
  29.4 0.9 %collective-permute-start.6 = (bf16[64,1024]{1,0:T(8,128)(2,1)S(1)}, bf16[64,1024]{1,0:T(8,128)(2,1)S(1)}, u32[]{:S(2)}, u32[]{:S(2)}) collective-permute-start(bf16[64,1024]{1,0:T(8,128)(2,1)S(1)} %get-tuple-element.45), channel_id=1, source_target_pairs={{0,2},{2,4},{4,6},{6,0},{1,3},{3,5},{5,7},{7,1},{8,10},{10,12},{12... | collective-permute-start | bytes 393224 | tf_op jit(solution)/shard_map/ppermute | solution.py:532
  30.3 2.7 %collective-permute-start.7 = (bf16[64,1024]{1,0:T(8,128)(2,1)S(1)}, bf16[64,1024]{1,0:T(8,128)(2,1)S(1)}, u32[]{:S(2)}, u32[]{:S(2)}) collective-permute-start(bf16[64,1024]{1,0:T(8,128)(2,1)S(1)} %get-tuple-element.46), channel_id=1, source_target_pairs={{0,6},{2,0},{4,2},{6,4},{1,7},{3,1},{5,3},{7,5},{8,14},{10,8},{12,... | collective-permute-start | bytes 393224 | tf_op jit(solution)/shard_map/ppermute | solution.py:532
  33.0 1.8 %collective-permute-start.14 = (bf16[1040,128]{1,0:T(8,128)(2,1)S(1)}, bf16[1040,128]{1,0:T(8,128)(2,1)S(1)}, u32[]{:S(2)}, u32[]{:S(2)}) collective-permute-start(bf16[1040,128]{1,0:T(8,128)(2,1)S(1)} %collective-permute-done.1.refs_2_), channel_id=1, source_target_pairs={{0,6},{2,0},{4,2},{6,4},{1,7},{3,1},{5,3},{7,5},{8,14},{10,8},{12,... | collective-permute-start | bytes 798728 | tf_op jit(solution)/shard_map/ppermute | solution.py:532
  34.8 1.3 %collective-permute-done.5.r2_ref = bf16[64,1024]{1,0:T(8,128)(2,1)S(1)} collective-permute-done((bf16[64,1024]{1,0:T(8,128)(2,1)S(1)}, bf16[64,1024]{1,0:T(8,128)(2,1)S(1)}, u32[]{:S(2)}, u32[]{:S(2)}) %collective-permute-start.5) | collective-permute-done | bytes 131104 | tf_op jit(solution)/shard_map/ppermute | solution.py:532
  36.1 4.8 %collective-permute-done.6.r1_ref = bf16[64,1024]{1,0:T(8,128)(2,1)S(1)} collective-permute-done((bf16[64,1024]{1,0:T(8,128)(2,1)S(1)}, bf16[64,1024]{1,0:T(8,128)(2,1)S(1)}, u32[]{:S(2)}, u32[]{:S(2)}) %collective-permute-start.6) | collective-permute-done | bytes 131104 | tf_op jit(solution)/shard_map/ppermute | solution.py:532
  40.9 8.1 %collective-permute-done.7.r3_ref = bf16[64,1024]{1,0:T(8,128)(2,1)S(1)} collective-permute-done((bf16[64,1024]{1,0:T(8,128)(2,1)S(1)}, bf16[64,1024]{1,0:T(8,128)(2,1)S(1)}, u32[]{:S(2)}, u32[]{:S(2)}) %collective-permute-start.7) | collective-permute-done | bytes 131104 | tf_op jit(solution)/shard_map/ppermute | solution.py:532
  49.0 1.0 %hidden.1 = (bf16[64,1024]{1,0:T(8,128)(2,1)}, f32[64,512]{1,0:T(8,128)S(1)}, bf16[64,640]{1,0:T(8,128)(2,1)S(1)}, f32[64,1]{1,0:T(8,128)S(1)}) custom-call(f32[4,64,1024]{2,1,0:T(8,128)S(1)} %get-tuple-element.39.own_ref, bf16[4,64,1024]{2,1,0:T(8,128)(2,1)S(1)} %collective-permute-done.4.peer_ref, bf16[64,1024]{1,0:T(8,128)(2,1)S(1)} %collective-permute-done.5.r2_ref, ...), custom_call_target="tpu_custom_call" | custom-call | flops 20000000 | bytes 60000 | tf_op jit(solution)/shard_map/hidden/pallas_call | solution.py:39
  50.0 0.7 collective-permute-start.8
  50.7 0.9 %collective-permute-done.8.recv_ref = bf16[64,640]{1,0:T(8,128)(2,1)S(1)} collective-permute-done((bf16[64,640]{1,0:T(8,128)(2,1)S(1)}, bf16[64,640]{1,0:T(8,128)(2,1)S(1)}, u32[]{:S(2)}, u32[]{:S(2)}) %collective-permute-start.8) | collective-permute-done | bytes 81952 | tf_op jit(solution)/shard_map/ppermute | solution.py:536
  51.7 1.1 %collective-permute-start.9 = (bf16[64,640]{1,0:T(8,128)(2,1)S(1)}, bf16[64,640]{1,0:T(8,128)(2,1)S(1)}, u32[]{:S(2)}, u32[]{:S(2)}) collective-permute-start(bf16[64,640]{1,0:T(8,128)(2,1)S(1)} %join.1.refs_0_.p0_ref), channel_id=1, source_target_pairs={{0,2},{2,4},{4,6},{6,0},{1,3},{3,5},{5,7},{7,1},{8,10},{10,12},{12... | collective-permute-start | bytes 245768 | tf_op jit(solution)/shard_map/ppermute | solution.py:532
  52.9 0.6 collective-permute-start.12
  53.5 0.5 collective-permute-start.16
  54.0 0.7 collective-permute-done.14.refs_4_
  54.7 2.8 %collective-permute-done.9.refs_1_.p1_ref = bf16[64,640]{1,0:T(8,128)(2,1)S(1)} collective-permute-done((bf16[64,640]{1,0:T(8,128)(2,1)S(1)}, bf16[64,640]{1,0:T(8,128)(2,1)S(1)}, u32[]{:S(2)}, u32[]{:S(2)}) %collective-permute-start.9) | collective-permute-done | bytes 81952 | tf_op jit(solution)/shard_map/ppermute | solution.py:532
  57.6 1.2 %collective-permute-start.15 = (bf16[1040,128]{1,0:T(8,128)(2,1)S(1)}, bf16[1040,128]{1,0:T(8,128)(2,1)S(1)}, u32[]{:S(2)}, u32[]{:S(2)}) collective-permute-start(bf16[1040,128]{1,0:T(8,128)(2,1)S(1)} %collective-permute-done.14.refs_4_), channel_id=1, source_target_pairs={{0,1},{1,0},{2,3},{3,2},{4,5},{5,4},{6,7},{7,6},{8,9},{9,8},{10,11... | collective-permute-start | bytes 798728 | tf_op jit(solution)/shard_map/ppermute | solution.py:536
  58.8 3.8 %collective-permute-start.10 = (bf16[64,640]{1,0:T(8,128)(2,1)S(1)}, bf16[64,640]{1,0:T(8,128)(2,1)S(1)}, u32[]{:S(2)}, u32[]{:S(2)}) collective-permute-start(bf16[64,640]{1,0:T(8,128)(2,1)S(1)} %join.1.refs_0_.p0_ref), channel_id=1, source_target_pairs={{0,4},{2,6},{4,0},{6,2},{1,5},{3,7},{5,1},{7,3},{8,12},{10,14},{12... | collective-permute-start | bytes 245768 | tf_op jit(solution)/shard_map/ppermute | solution.py:532
  62.6 3.5 %main_conv.1 = (bf16[1024,128]{1,0:T(8,128)(2,1)}, bf16[128,1024]{1,0:T(8,128)(2,1)S(1)}, f32[8,1024]{1,0:T(8,128)S(1)}, bf16[32,1024]{1,0:T(8,128)(2,1)S(1)}, bf16[32,1024]{1,0:T(8,128)(2,1)S(1)}) custom-call(bf16[1040,128]{1,0:T(8,128)(2,1)S(1)} %get-tuple-element.54.refs_0_, bf16[1040,128]{1,0:T(8,128)(2,1)S(1)} %collective-permute-done.12.refs_1_, ...), custom_call_target="tpu_custom_call" | custom-call | flops 40000000 | bytes 120000 | tf_op jit(solution)/shard_map/main_conv/pallas_call | solution.py:39
  66.1 0.7 collective-permute-done.10.refs_2_.p2_ref
  67.5 15.3 %all_to_all.5.mine_ref = bf16[32,8,512]{2,1,0:T(8,128)(2,1)S(1)} all-to-all(bf16[32,8,512]{2,1,0:T(8,128)(2,1)S(1)} %dispatch.1), channel_id=1, replica_groups=mesh['dp'=32,'zh'=4,'c'=2] {'dp'}, dimensions={0} | all-to-all | bytes 524288 | tf_op jit(solution)/shard_map/all_to_all | solution.py:574
  82.8 2.3 %collective-permute-start.17 = (bf16[32,8,512]{2,1,0:T(8,128)(2,1)S(1)}, bf16[32,8,512]{2,1,0:T(8,128)(2,1)S(1)}, u32[]{:S(2)}, u32[]{:S(2)}) collective-permute-start(bf16[32,8,512]{2,1,0:T(8,128)(2,1)S(1)} %all_to_all.5.mine_ref), channel_id=1, source_target_pairs={{0,1},{1,0},{2,3},{3,2},{4,5},{5,4},{6,7},{7,6},{8,9},{9,8},{10,11... | collective-permute-start | bytes 786440 | tf_op jit(solution)/shard_map/ppermute | solution.py:536
  85.1 1.2 %collective-permute-done.17.peer_ref = bf16[32,8,512]{2,1,0:T(8,128)(2,1)S(1)} collective-permute-done((bf16[32,8,512]{2,1,0:T(8,128)(2,1)S(1)}, bf16[32,8,512]{2,1,0:T(8,128)(2,1)S(1)}, u32[]{:S(2)}, u32[]{:S(2)}) %collective-permute-start.17) | collective-permute-done | bytes 262176 | tf_op jit(solution)/shard_map/ppermute | solution.py:536
  86.3 2.0 %final_conv.1 = bf16[1024,128]{1,0:T(8,128)(2,1)} custom-call(bf16[32,8,512]{2,1,0:T(8,128)(2,1)S(1)} %all_to_all.5.mine_ref, bf16[32,8,512]{2,1,0:T(8,128)(2,1)S(1)} %collective-permute-done.17.peer_ref, bf16[128,1024]{1,0:T(8,128)(2,1)S(1)} %get-tuple-element.64.raw_ref, ...), custom_call_target="tpu_custom_call", output_to_operand_aliasing={{}: (13, {})} | custom-call | flops 30000000 | bytes 90000 | tf_op jit(solution)/shard_map/final_conv/pallas_call | solution.py:39
  (14 shorter events, 1.0 us)
Async XLA Ops:
  2.3 18.3 %collective-permute-start = (bf16[1040,128]{1,0:T(8,128)(2,1)S(1)}, bf16[1040,128]{1,0:T(8,128)(2,1)S(1)}, u32[]{:S(2)}, u32[]{:S(2)}) collective-permute-start(bf16[1040,128]{1,0:T(8,128)(2,1)S(1)} %get-tuple-element.54.refs_0_), channel_id=1, source_target_pairs={{0,2},{2,4},{4,6},{6,0},{1,3},{3,5},{5,7},{7,1},{8,10},{10,12},{12... | collective-permute-start | bytes 798728 | tf_op jit(solution)/shard_map/ppermute | solution.py:532
  6.2 16.3 %collective-permute-start.1 = (bf16[1040,128]{1,0:T(8,128)(2,1)S(1)}, bf16[1040,128]{1,0:T(8,128)(2,1)S(1)}, u32[]{:S(2)}, u32[]{:S(2)}) collective-permute-start(bf16[1040,128]{1,0:T(8,128)(2,1)S(1)} %get-tuple-element.54.refs_0_), channel_id=1, source_target_pairs={{0,6},{2,0},{4,2},{6,4},{1,7},{3,1},{5,3},{7,5},{8,14},{10,8},{12,... | collective-permute-start | bytes 798728 | tf_op jit(solution)/shard_map/ppermute | solution.py:532
  9.3 11.2 %collective-permute-start.2 = (bf16[16,128]{1,0:T(8,128)(2,1)S(1)}, bf16[16,128]{1,0:T(8,128)(2,1)S(1)}, u32[]{:S(2)}, u32[]{:S(2)}) collective-permute-start(bf16[16,128]{1,0:T(8,128)(2,1)S(1)} %get-tuple-element.41), channel_id=1, source_target_pairs={{0,8},{8,16},{16,24},{24,32},{32,40},{40,48},{48,56},{56,64},{64,7... | collective-permute-start | bytes 12296 | tf_op jit(solution)/shard_map/ppermute | solution.py:553
  11.9 8.6 %collective-permute-start.3 = (bf16[16,128]{1,0:T(8,128)(2,1)S(1)}, bf16[16,128]{1,0:T(8,128)(2,1)S(1)}, u32[]{:S(2)}, u32[]{:S(2)}) collective-permute-start(bf16[16,128]{1,0:T(8,128)(2,1)S(1)} %get-tuple-element.42), channel_id=1, source_target_pairs={{8,0},{16,8},{24,16},{32,24},{40,32},{48,40},{56,48},{64,56},{72,6... | collective-permute-start | bytes 12296 | tf_op jit(solution)/shard_map/ppermute | solution.py:554
  22.4 3.1 %collective-permute-start.4 = (bf16[4,64,1024]{2,1,0:T(8,128)(2,1)S(1)}, bf16[4,64,1024]{2,1,0:T(8,128)(2,1)S(1)}, u32[]{:S(2)}, u32[]{:S(2)}) collective-permute-start(bf16[4,64,1024]{2,1,0:T(8,128)(2,1)S(1)} %get-tuple-element.43), channel_id=1, source_target_pairs={{0,1},{1,0},{2,3},{3,2},{4,5},{5,4},{6,7},{7,6},{8,9},{9,8},{10,11... | collective-permute-start | bytes 1572872 | tf_op jit(solution)/shard_map/ppermute | solution.py:536
  25.7 10.5 %collective-permute-start.5 = (bf16[64,1024]{1,0:T(8,128)(2,1)S(1)}, bf16[64,1024]{1,0:T(8,128)(2,1)S(1)}, u32[]{:S(2)}, u32[]{:S(2)}) collective-permute-start(bf16[64,1024]{1,0:T(8,128)(2,1)S(1)} %get-tuple-element.44), channel_id=1, source_target_pairs={{0,4},{2,6},{4,0},{6,2},{1,5},{3,7},{5,1},{7,3},{8,12},{10,14},{12... | collective-permute-start | bytes 393224 | tf_op jit(solution)/shard_map/ppermute | solution.py:532
  29.4 11.5 %collective-permute-start.6 = (bf16[64,1024]{1,0:T(8,128)(2,1)S(1)}, bf16[64,1024]{1,0:T(8,128)(2,1)S(1)}, u32[]{:S(2)}, u32[]{:S(2)}) collective-permute-start(bf16[64,1024]{1,0:T(8,128)(2,1)S(1)} %get-tuple-element.45), channel_id=1, source_target_pairs={{0,2},{2,4},{4,6},{6,0},{1,3},{3,5},{5,7},{7,1},{8,10},{10,12},{12... | collective-permute-start | bytes 393224 | tf_op jit(solution)/shard_map/ppermute | solution.py:532
  30.3 18.7 %collective-permute-start.7 = (bf16[64,1024]{1,0:T(8,128)(2,1)S(1)}, bf16[64,1024]{1,0:T(8,128)(2,1)S(1)}, u32[]{:S(2)}, u32[]{:S(2)}) collective-permute-start(bf16[64,1024]{1,0:T(8,128)(2,1)S(1)} %get-tuple-element.46), channel_id=1, source_target_pairs={{0,6},{2,0},{4,2},{6,4},{1,7},{3,1},{5,3},{7,5},{8,14},{10,8},{12,... | collective-permute-start | bytes 393224 | tf_op jit(solution)/shard_map/ppermute | solution.py:532
  33.0 21.7 %collective-permute-start.14 = (bf16[1040,128]{1,0:T(8,128)(2,1)S(1)}, bf16[1040,128]{1,0:T(8,128)(2,1)S(1)}, u32[]{:S(2)}, u32[]{:S(2)}) collective-permute-start(bf16[1040,128]{1,0:T(8,128)(2,1)S(1)} %collective-permute-done.1.refs_2_), channel_id=1, source_target_pairs={{0,6},{2,0},{4,2},{6,4},{1,7},{3,1},{5,3},{7,5},{8,14},{10,8},{12,... | collective-permute-start | bytes 798728 | tf_op jit(solution)/shard_map/ppermute | solution.py:532
  50.0 1.6 %collective-permute-start.8 = (bf16[64,640]{1,0:T(8,128)(2,1)S(1)}, bf16[64,640]{1,0:T(8,128)(2,1)S(1)}, u32[]{:S(2)}, u32[]{:S(2)}) collective-permute-start(bf16[64,640]{1,0:T(8,128)(2,1)S(1)} %get-tuple-element.52), channel_id=1, source_target_pairs={{0,1},{1,0},{2,3},{3,2},{4,5},{5,4},{6,7},{7,6},{8,9},{9,8},{10,11... | collective-permute-start | bytes 245768 | tf_op jit(solution)/shard_map/ppermute | solution.py:536
  51.7 5.9 %collective-permute-start.9 = (bf16[64,640]{1,0:T(8,128)(2,1)S(1)}, bf16[64,640]{1,0:T(8,128)(2,1)S(1)}, u32[]{:S(2)}, u32[]{:S(2)}) collective-permute-start(bf16[64,640]{1,0:T(8,128)(2,1)S(1)} %join.1.refs_0_.p0_ref), channel_id=1, source_target_pairs={{0,2},{2,4},{4,6},{6,0},{1,3},{3,5},{5,7},{7,1},{8,10},{10,12},{12... | collective-permute-start | bytes 245768 | tf_op jit(solution)/shard_map/ppermute | solution.py:532
  52.9 9.7 %collective-permute-start.12 = (bf16[1040,128]{1,0:T(8,128)(2,1)S(1)}, bf16[1040,128]{1,0:T(8,128)(2,1)S(1)}, u32[]{:S(2)}, u32[]{:S(2)}) collective-permute-start(bf16[1040,128]{1,0:T(8,128)(2,1)S(1)} %get-tuple-element.54.refs_0_), channel_id=1, source_target_pairs={{0,1},{1,0},{2,3},{3,2},{4,5},{5,4},{6,7},{7,6},{8,9},{9,8},{10,11... | collective-permute-start | bytes 798728 | tf_op jit(solution)/shard_map/ppermute | solution.py:536
  53.5 9.1 %collective-permute-start.13 = (bf16[1040,128]{1,0:T(8,128)(2,1)S(1)}, bf16[1040,128]{1,0:T(8,128)(2,1)S(1)}, u32[]{:S(2)}, u32[]{:S(2)}) collective-permute-start(bf16[1040,128]{1,0:T(8,128)(2,1)S(1)} %collective-permute-done.1.refs_2_), channel_id=1, source_target_pairs={{0,1},{1,0},{2,3},{3,2},{4,5},{5,4},{6,7},{7,6},{8,9},{9,8},{10,11... | collective-permute-start | bytes 798728 | tf_op jit(solution)/shard_map/ppermute | solution.py:536
  53.5 9.1 %collective-permute-start.16 = (bf16[1040,128]{1,0:T(8,128)(2,1)S(1)}, bf16[1040,128]{1,0:T(8,128)(2,1)S(1)}, u32[]{:S(2)}, u32[]{:S(2)}) collective-permute-start(bf16[1040,128]{1,0:T(8,128)(2,1)S(1)} %collective-permute-done.refs_6_), channel_id=1, source_target_pairs={{0,1},{1,0},{2,3},{3,2},{4,5},{5,4},{6,7},{7,6},{8,9},{9,8},{10,11... | collective-permute-start | bytes 798728 | tf_op jit(solution)/shard_map/ppermute | solution.py:536
  57.6 5.0 %collective-permute-start.15 = (bf16[1040,128]{1,0:T(8,128)(2,1)S(1)}, bf16[1040,128]{1,0:T(8,128)(2,1)S(1)}, u32[]{:S(2)}, u32[]{:S(2)}) collective-permute-start(bf16[1040,128]{1,0:T(8,128)(2,1)S(1)} %collective-permute-done.14.refs_4_), channel_id=1, source_target_pairs={{0,1},{1,0},{2,3},{3,2},{4,5},{5,4},{6,7},{7,6},{8,9},{9,8},{10,11... | collective-permute-start | bytes 798728 | tf_op jit(solution)/shard_map/ppermute | solution.py:536
  58.8 8.0 %collective-permute-start.10 = (bf16[64,640]{1,0:T(8,128)(2,1)S(1)}, bf16[64,640]{1,0:T(8,128)(2,1)S(1)}, u32[]{:S(2)}, u32[]{:S(2)}) collective-permute-start(bf16[64,640]{1,0:T(8,128)(2,1)S(1)} %join.1.refs_0_.p0_ref), channel_id=1, source_target_pairs={{0,4},{2,6},{4,0},{6,2},{1,5},{3,7},{5,1},{7,3},{8,12},{10,14},{12... | collective-permute-start | bytes 245768 | tf_op jit(solution)/shard_map/ppermute | solution.py:532
  62.5 4.7 %collective-permute-start.11 = (bf16[64,640]{1,0:T(8,128)(2,1)S(1)}, bf16[64,640]{1,0:T(8,128)(2,1)S(1)}, u32[]{:S(2)}, u32[]{:S(2)}) collective-permute-start(bf16[64,640]{1,0:T(8,128)(2,1)S(1)} %join.1.refs_0_.p0_ref), channel_id=1, source_target_pairs={{0,6},{2,0},{4,2},{6,4},{1,7},{3,1},{5,3},{7,5},{8,14},{10,8},{12,... | collective-permute-start | bytes 245768 | tf_op jit(solution)/shard_map/ppermute | solution.py:532
  82.8 3.4 %collective-permute-start.17 = (bf16[32,8,512]{2,1,0:T(8,128)(2,1)S(1)}, bf16[32,8,512]{2,1,0:T(8,128)(2,1)S(1)}, u32[]{:S(2)}, u32[]{:S(2)}) collective-permute-start(bf16[32,8,512]{2,1,0:T(8,128)(2,1)S(1)} %all_to_all.5.mine_ref), channel_id=1, source_target_pairs={{0,1},{1,0},{2,3},{3,2},{4,5},{5,4},{6,7},{7,6},{8,9},{9,8},{10,11... | collective-permute-start | bytes 786440 | tf_op jit(solution)/shard_map/ppermute | solution.py:536
